TPU v7x, 512 devices: a whole 4x4x16 slice. The times are simulated.
512 devices in a mesh: section: 16 (over x, z_hi, core), tensor: 32 (over z_lo, y).
Axes of the slice: x: 4, y: 4, z: 16 (z_hi: 2, z_lo: 8; z = z_hi * 8 + z_lo), core: 2. Of those that a mesh axis runs over, the one named last changes fastest.
Arguments:
- context: bfloat16 [16, 256, 4096], P('section', None, 'tensor'), may hold values from -6 to 6
- out_weight: bfloat16 [16, 4096, 8192], P('section', 'tensor'), may hold values from -0.09375 to 0.09375
- residual: bfloat16 [16, 256, 8192], P('section', None, 'tensor'), may hold values from -36 to 36
- gain: float32 [16, 8192], P('section', 'tensor'), may hold values from 0.1 to 1.9
- q_weight: bfloat16 [16, 8192, 4096], P('section', None, 'tensor'), may hold values from -0.044194174 to 0.044194174
- kv_weight: bfloat16 [16, 8192, 1024], P('section', None, 'tensor'), may hold values from -0.044194174 to 0.044194174
Outputs:
- attended: bfloat16 [16, 256, 4096], P('section', None, 'tensor')
All inputs are finite; a program needn't handle non-finite values.
Results may differ from a plain program's by a relative error of at most 0.033.
Values may be sent and summed in bfloat16 or wider, within the bound.
No kernel may reach another device: no remote copies, remote signals or barrier semaphores. Data moves between devices by JAX's collectives and lax.ppermute only.
A program may use at most 64 MiB of HBM per device.

v0:
```python
import jax
import jax.numpy as jnp
from jax import lax
from jax.sharding import PartitionSpec as P

GROUP = 8


THETA = 500000.0


def passed_along(block, axis, distance):
    devices = range(lax.axis_size(axis))
    route = [((i - distance) % len(devices), i) for i in devices]
    return lax.ppermute(block, axis, route)


def rotate(inputs, positions):
    half_width = inputs.shape[-1] // 2
    frequency = THETA ** (-(jnp.arange(half_width).astype(jnp.float32) * 2.0 / inputs.shape[-1]))
    angles = positions[:, None] * frequency[None, :]
    cosine = jnp.cos(angles)[:, None, :]
    sine_part = jnp.sin(angles)[:, None, :]
    first_half = inputs[..., :half_width]
    second_half = inputs[..., half_width:]
    return jnp.concatenate(
        [
            first_half * cosine - second_half * sine_part,
            second_half * cosine + first_half * sine_part,
        ],
        axis=-1,
    )


def on_device(context, out_weight, residual, gain, q_weight, kv_weight):
    local_context = context[0]
    local_out = out_weight[0]
    terms = jnp.dot(local_context, local_out, preferred_element_type=jnp.float32)
    summed = lax.psum_scatter(
        terms.astype(jnp.bfloat16), "tensor", scatter_dimension=1, tiled=True
    ).astype(jnp.float32)
    combined = (residual[0].astype(jnp.float32) + summed).astype(jnp.bfloat16)
    section_gain = gain[0]
    query_cols = q_weight[0]
    pair_cols = kv_weight[0]
    head_size = query_cols.shape[1]
    length = combined.shape[0]
    gathered = lax.all_gather(combined, "tensor", axis=1, tiled=True)
    shifted = passed_along(gathered, "section", 1)
    full_gain = lax.all_gather(section_gain, "tensor", axis=0, tiled=True)
    values_f = shifted.astype(jnp.float32)
    normed = (
        values_f
        * lax.rsqrt(jnp.mean(values_f * values_f, axis=-1, keepdims=True) + 1e-05)
        * full_gain[None, :]
    ).astype(jnp.bfloat16)
    query_proj = jnp.dot(normed, query_cols, preferred_element_type=jnp.float32)
    pair_proj = jnp.dot(normed, pair_cols, preferred_element_type=jnp.float32)
    positions = jnp.arange(length).astype(jnp.float32)
    queries = rotate(query_proj[:, None, :], positions)[:, 0].astype(jnp.bfloat16)
    pair_part = pair_proj.astype(jnp.bfloat16)
    all_pairs = lax.all_gather(pair_part, "tensor", axis=1, tiled=True)
    group_count = lax.axis_size("tensor")
    feature_share = head_size // group_count
    kv_total = pair_cols.shape[1] * group_count // (2 * head_size)
    group_index = lax.axis_index("tensor") // GROUP
    split_cols = all_pairs.reshape(length, group_count, kv_total, 2 * feature_share)
    picked = lax.dynamic_index_in_dim(split_cols, group_index, 2, keepdims=False)
    picked = jnp.transpose(
        picked.reshape(length, group_count, 2, feature_share), (0, 2, 1, 3)
    ).reshape(length, 2, head_size)
    key_rows = rotate(picked[:, 0:1].astype(jnp.float32), positions)[:, 0].astype(jnp.bfloat16)
    values = picked[:, 1]
    scores = jnp.einsum(
        "sd,td->st", queries, key_rows, preferred_element_type=jnp.float32
    ) * head_size ** (-0.5)
    order = jnp.arange(length)
    causal = order[:, None] >= order[None, :]
    scores = jnp.where(causal, scores, -1e30)
    softmax_weights = jax.nn.softmax(scores, axis=-1).astype(jnp.bfloat16)
    attended = jnp.dot(softmax_weights, values, preferred_element_type=jnp.float32).astype(
        jnp.bfloat16
    )
    return attended[None]


def solution(mesh):
    placed = (
        P("section", None, "tensor"),
        P("section", "tensor", None),
        P("section", None, "tensor"),
        P("section", "tensor"),
        P("section", None, "tensor"),
        P("section", None, "tensor"),
    )
    return jax.shard_map(
        on_device,
        mesh=mesh,
        in_specs=placed,
        out_specs=P("section", None, "tensor"),
        check_vma=False,
    )
```

profile of v0, /device:TPU:1, one launch (start us, length us, event | category | flops | bytes accessed | tf_op | source)
XLA Modules:
  0.0 821.7 jit_solution(9606047402175932910)
XLA Ops:
  6.5 0.0 copy-start
  6.5 0.0 reduce-scatter.2.cloned.1.call-start
  6.5 1.6 copy-done
  8.1 4.0 convolution_convert_fusion
  12.1 0.0 reduce-scatter.2.cloned.1.call-update
  12.2 0.0 all-gather.3.cloned.1.call-start
  12.2 227.8 %reduce-scatter.2.cloned.1.call-done = bf16[256,256]{1,0:T(8,128)(2,1)} async-done(((bf16[256,8192]{1,0:T(8,128)(2,1)}), bf16[256,256]{1,0:T(8,128)(2,1)}) %reduce-scatter.2.cloned.1.call-update) | async-done | bytes 131088 | tf_op jit(solution)/shard_map/reduce_scatter | solution.py:39
  240.1 0.0 copy-done.1
  240.1 1.6 fusion.20
  241.7 0.0 all-gather.3.cloned.1.call-update
  241.7 193.1 %all-gather.3.cloned.1.call-done = bf16[256,8192]{1,0:T(8,128)(2,1)} async-done(((bf16[256,256]{1,0:T(8,128)(2,1)}), bf16[256,8192]{1,0:T(8,128)(2,1)}) %all-gather.3.cloned.1.call-update) | async-done | bytes 4194320 | tf_op jit(solution)/shard_map/all_gather | solution.py:48
  434.8 21.0 %collective-permute-start = (bf16[256,8192]{1,0:T(8,128)(2,1)}, bf16[256,8192]{1,0:T(8,128)(2,1)}, u32[]{:S(2)}, u32[]{:S(2)}) collective-permute-start(bf16[256,8192]{1,0:T(8,128)(2,1)} %all-gather.3.cloned.1.call-done), channel_id=1, source_target_pairs={{480,0},{0,32},{32,64},{64,96},{96,128},{128,160},{160,192},{192,2... | collective-permute-start | bytes 12582920 | tf_op jit(solution)/shard_map/ppermute | solution.py:15
  455.8 0.0 copy-done.2
  455.8 245.5 %all-gather = f32[1,8192]{1,0:T(1,128)S(1)} all-gather(f32[1,256]{1,0:T(1,128)S(1)} %copy-done.2), channel_id=2, replica_groups=mesh['section'=16,'tensor'=32] {'tensor'}, dimensions={1}, use_global_device_ids=true | all-gather | bytes 33792 | tf_op jit(solution)/shard_map/all_gather | solution.py:50
  701.3 0.0 collective-permute-done
  701.4 3.1 fusion
  704.5 3.6 fusion.16
  708.1 100.4 %all_gather.11 = bf16[256,1024]{0,1:T(8,128)(2,1)S(1)} all-gather(bf16[256,32]{0,1:T(8,128)(2,1)S(1)} %fusion.16), channel_id=1, replica_groups=mesh['section'=16,'tensor'=32] {'tensor'}, dimensions={1}, use_global_device_ids=true | all-gather | bytes 540672 | tf_op jit(solution)/shard_map/all_gather | solution.py:62
  808.5 0.1 copy.8
  808.7 4.6 fusion.10
  813.3 0.3 fusion.46
  813.7 0.3 fusion.50
  813.9 0.1 fusion.21
  814.0 0.9 fusion.15
  (11 shorter events, 0.1 us)
Async XLA Ops:
  6.5 1.6 copy-start
  6.5 233.5 %copy-start.1 = (bf16[1,256,256]{2,1,0:T(8,128)(2,1)S(1)}, bf16[1,256,256]{2,1,0:T(8,128)(2,1)}, u32[]{:S(2)}) copy-start(bf16[1,256,256]{2,1,0:T(8,128)(2,1)} %param.8) | copy-start | bytes 393220
  6.5 449.3 %copy-start.2 = (f32[1,256]{1,0:T(1,128)S(1)}, f32[1,256]{1,0:T(1,128)}, u32[]{:S(2)}) copy-start(f32[1,256]{1,0:T(1,128)} %param.9) | copy-start | bytes 3076
  6.5 233.5 %reduce-scatter.2.cloned.1.call-start = ((), (), s32[]{:S(2)}) async-start(), calls=%async_computation.1 | async-start | bytes 4325376 | tf_op jit(solution)/shard_map/reduce_scatter | solution.py:39
  12.1 692.3 %copy-start.3 = (bf16[1,8192,32]{1,2,0:T(8,128)(2,1)S(1)}, bf16[1,8192,32]{1,2,0:T(8,128)(2,1)}, u32[]{:S(2)}) copy-start(bf16[1,8192,32]{1,2,0:T(8,128)(2,1)} %param.11) | copy-start | bytes 1572868
  12.2 422.6 %all-gather.3.cloned.1.call-start = ((), (), s32[]{:S(2)}) async-start(), calls=%async_computation.2 | async-start | bytes 4325376 | tf_op jit(solution)/shard_map/all_gather | solution.py:48
  434.8 266.5 %collective-permute-start = (bf16[256,8192]{1,0:T(8,128)(2,1)}, bf16[256,8192]{1,0:T(8,128)(2,1)}, u32[]{:S(2)}, u32[]{:S(2)}) collective-permute-start(bf16[256,8192]{1,0:T(8,128)(2,1)} %all-gather.3.cloned.1.call-done), channel_id=1, source_target_pairs={{480,0},{0,32},{32,64},{64,96},{96,128},{128,160},{160,192},{192,2... | collective-permute-start | bytes 12582920 | tf_op jit(solution)/shard_map/ppermute | solution.py:15
Sparse Core Ops, SparseCore 0:
  12.3 227.7 reduce-scatter.1
  242.1 192.6 all-gather.2
where the time goes:
time: 822 us
  waiting for transfers between devices  421 us (51%)
  blocking collectives  346 us (42%)
  starting transfers between devices  21 us (3%)
  between operations  13.5 us (2%)
  matrix products  13.4 us (2%)
    all_gather x1, blocking collectives, on_device(): full_gain = lax.all_gather(section_gain, 'tensor', axis=0, tiled=True)  246 us
    reduce_scatter x1, waiting for transfers between devices, on_device(): lax.psum_scatter(terms.astype(jnp.bfloat16), 'tensor', scatter_dimension=...  228 us
    all_gather x1, waiting for transfers between devices, on_device(): gathered = lax.all_gather(combined, 'tensor', axis=1, tiled=True)  193 us
    all_gather x1, blocking collectives, on_device(): all_pairs = lax.all_gather(pair_part, 'tensor', axis=1, tiled=True)  100 us
    ppermute x1, starting transfers between devices, passed_along(): return lax.ppermute(block, axis, route)  21 us
  transfers between devices with their start and end apart: 3, of which 2 were waited for; matrix products, arithmetic and copies ran while one was open for 0% of the time, Pallas kernels for 0%

commit v1 on v0

v1 whole, which is shorter than its diff:
```python
import jax
import jax.numpy as jnp
from jax import lax
from jax.sharding import Mesh, PartitionSpec as P

THETA = 500000.0
ROWS, COLS = 4, 8
BF16, F32 = jnp.bfloat16, jnp.float32


def contract(lhs, rhs, lhs_dim, rhs_dim):
    return lax.dot_general(
        lhs, rhs, (((lhs_dim,), (rhs_dim,)), ((), ())), preferred_element_type=F32
    )


def exchange(pieces, axis):
    return lax.all_to_all(pieces, axis, 0, 0, tiled=True)


def turn(rows, cosine, sine):
    half = rows.shape[0] // 2
    first, second = rows[:half], rows[half:]
    return jnp.concatenate(
        [first * cosine - second * sine, second * cosine + first * sine], axis=0
    )


def stats_rows(total):
    high = lax.reduce_precision(total, 8, 7)
    low = total - high
    rows = jnp.stack([high, low]).astype(BF16)
    return jnp.concatenate([rows, jnp.zeros((14, total.shape[0]), BF16)], axis=0)


def on_device(context, out_weight, residual, gain, q_weight, kv_weight):
    tokens, head = context.shape[1:]
    width = out_weight.shape[2]
    part = width // (ROWS * COLS)
    block = ROWS * part

    out_cols = out_weight[0].reshape(head, ROWS, COLS, part).transpose(2, 0, 1, 3)
    out_cols = out_cols.reshape(COLS, head, block)
    own = jnp.broadcast_to(context[0].T[None], (COLS, head, tokens))
    got = exchange(jnp.concatenate([out_cols, own], axis=2), "a")
    row_weight = got[:, :, :block].reshape(COLS * head, block)
    row_context = got[:, :, block:].reshape(COLS * head, tokens)
    terms = contract(row_weight, row_context, 0, 0).astype(BF16)

    q_rows = q_weight[0].reshape(ROWS, COLS, part, head).transpose(1, 0, 2, 3)
    q_block = exchange(q_rows.reshape(COLS, block, head), "a")
    kv_rows = kv_weight[0].T.reshape(ROWS, 8, width)
    kv_rows = exchange(kv_rows, "b")
    kv_rows = kv_rows.reshape(ROWS, 8, ROWS, COLS, part).transpose(3, 0, 1, 2, 4)
    kv_block = exchange(kv_rows.reshape(COLS, ROWS * 8, block), "a")
    kv_block = kv_block.reshape(COLS, ROWS, 2, 4, block).transpose(2, 1, 0, 3, 4)
    kv_block = kv_block.reshape(2 * head, block)

    terms = exchange(terms.reshape(ROWS, part, tokens), "b").astype(F32)
    handover = (residual[0].T.astype(F32) + jnp.sum(terms, axis=0)).astype(BF16)
    sections = lax.axis_size("section")
    received = lax.ppermute(
        handover, "section", [(i, (i + 1) % sections) for i in range(sections)]
    ).astype(F32)

    scaled = (received * gain[0][:, None]).astype(BF16)
    squares = stats_rows(jnp.sum(received * received, axis=0))
    gathered = lax.all_gather(jnp.concatenate([scaled, squares], axis=0), "b", axis=0)
    features = gathered[:, :part].reshape(block, tokens)
    squares = stats_rows(jnp.sum(gathered[:, part:part + 2].astype(F32), axis=(0, 1)))

    q_part = contract(q_block, features, 1, 0).astype(BF16)
    kv_part = contract(kv_block, features, 1, 0).astype(BF16)
    shared = jnp.concatenate([kv_part, squares], axis=0)
    shared = jnp.broadcast_to(shared[None], (COLS,) + shared.shape)
    summed = exchange(jnp.concatenate([q_part, shared], axis=1), "a").astype(F32)
    summed = jnp.sum(summed, axis=0)
    total = summed[3 * head] + summed[3 * head + 1]
    summed = summed[:3 * head] * lax.rsqrt(total / width + 1e-05)[None, :]

    positions = jnp.arange(tokens).astype(F32)
    frequency = THETA ** (-(jnp.arange(head // 2).astype(F32) * 2.0 / head))
    angles = frequency[:, None] * positions[None, :]
    cosine, sine = jnp.cos(angles), jnp.sin(angles)
    queries = turn(summed[:head], cosine, sine).astype(BF16)
    keys = summed[head:2 * head].astype(BF16).astype(F32)
    keys = turn(keys, cosine, sine).astype(BF16)
    values = summed[2 * head:].astype(BF16)
    scores = contract(queries, keys, 0, 0) * head ** (-0.5)
    order = jnp.arange(tokens)
    scores = jnp.where(order[:, None] >= order[None, :], scores, -1e30)
    softmax_weights = jax.nn.softmax(scores, axis=-1).astype(BF16)
    attended = contract(softmax_weights, values, 1, 1).astype(BF16)
    return attended[None]


def solution(mesh):
    sections = mesh.devices.shape[0]
    fine = Mesh(mesh.devices.reshape(sections, ROWS, COLS), ("section", "b", "a"))
    tensor = ("b", "a")
    placed = (
        P("section", None, tensor),
        P("section", tensor, None),
        P("section", None, tensor),
        P("section", tensor),
        P("section", None, tensor),
        P("section", None, tensor),
    )
    return jax.shard_map(
        on_device,
        mesh=fine,
        in_specs=placed,
        out_specs=P("section", None, tensor),
        check_vma=False,
    )
```

time: 822 us -> 210 us (0.26)
  the two profiles are of different devices: /device:TPU:1 before, /device:TPU:6 now
where the time goes in v1:
time: 210 us; the launch traced here: 208 us
  waiting for transfers between devices  120 us (57%)
  starting transfers between devices  35.7 us (17%)
  blocking collectives  28.3 us (13%)
  local copies, waits for them, and re-layouts  15.9 us (8%)
  other arithmetic  4.22 us (2%)
  matrix products  3.7 us (2%)
    all_to_all x6, waiting for transfers between devices, exchange(): return lax.all_to_all(pieces, axis, 0, 0, tiled=True)  90.7 us
    all_to_all x6, starting transfers between devices, exchange(): return lax.all_to_all(pieces, axis, 0, 0, tiled=True)  33.8 us
    ppermute x1, waiting for transfers between devices, on_device(): lax.ppermute(handover, 'section', [(i, (i + 1) % sections) for i in range...  29.1 us
    all_gather x1, blocking collectives, on_device(): lax.all_gather(jnp.concatenate([scaled, squares], axis=0), 'b', axis=0)  28.3 us
  transfers between devices with their start and end apart: 7, of which 6 were waited for; matrix products, arithmetic and copies ran while one was open for 9% of the time, Pallas kernels for 0%

profile of v1, /device:TPU:6, one launch (start us, length us, event | category | flops | bytes accessed | tf_op | source)
XLA Modules:
  0.0 207.9 jit_solution(548905245591516638)
XLA Ops:
  0.0 11.2 %all-to-all-start.3 = ((bf16[4,8,8192]{2,1,0:T(8,128)(2,1)}), bf16[4,8,8192]{2,1,0:T(8,128)(2,1)S(1)}, u32[]{:S(2)}, u32[]{:S(2)}) async-start(bf16[4,8,8192]{2,1,0:T(8,128)(2,1)} %bitcast.79), calls=%async_computation.3 | async-start | bytes 1048576 | tf_op jit(solution)/shard_map/all_to_all | solution.py:18
  11.2 2.2 %copy.34 = bf16[16,8,32,256]{3,2,1,0:T(8,128)(2,1)S(1)} copy(bf16[16,8,32,256]{3,1,2,0:T(8,128)(2,1)} %bitcast.70) | data formatting | bytes 4194304
  13.4 2.1 %copy.39 = bf16[128,4,8,256]{3,1,0,2:T(4,128)(2,1)} copy(bf16[128,4,8,256]{3,2,1,0:T(8,128)(2,1)S(1)} %bitcast.66) | data formatting | bytes 4194304 | tf_op jit(solution)/shard_map/reshape;squeeze | solution.py:42
  15.5 3.3 %reshape.75 = bf16[8,128,1024]{2,1,0:T(8,128)(2,1)S(1)} reshape(bf16[8,128,4,256]{3,2,1,0:T(4,128)(2,1)} %bitcast.65) | data formatting | bytes 4194304 | tf_op jit(solution)/shard_map/reshape | solution.py:43
  18.9 1.7 pad_maximum_fusion
  20.7 19.2 %all-to-all-done.3 = bf16[4,8,8192]{2,1,0:T(8,128)(2,1)S(1)} async-done(((bf16[4,8,8192]{2,1,0:T(8,128)(2,1)}), bf16[4,8,8192]{2,1,0:T(8,128)(2,1)S(1)}, u32[]{:S(2)}, u32[]{:S(2)}) %all-to-all-start.3) | async-done | bytes 524320 | tf_op jit(solution)/shard_map/all_to_all | solution.py:18
  39.9 4.5 %all-to-all-start = ((bf16[8,128,1280]{2,1,0:T(8,128)(2,1)}), bf16[8,128,1280]{2,1,0:T(8,128)(2,1)S(1)}, u32[]{:S(2)}, u32[]{:S(2)}) async-start(bf16[8,128,1280]{2,1,0:T(8,128)(2,1)} %pad_maximum_fusion), calls=%async_computation | async-start | bytes 5242880 | tf_op jit(solution)/shard_map/all_to_all | solution.py:18
  44.8 1.2 reshape.81
  45.9 28.3 %all-to-all-done = bf16[8,128,1280]{2,1,0:T(8,128)(2,1)S(1)} async-done(((bf16[8,128,1280]{2,1,0:T(8,128)(2,1)}), bf16[8,128,1280]{2,1,0:T(8,128)(2,1)S(1)}, u32[]{:S(2)}, u32[]{:S(2)}) %all-to-all-start) | async-done | bytes 2621472 | tf_op jit(solution)/shard_map/all_to_all | solution.py:18
  74.3 3.6 %all-to-all-start.4 = ((bf16[8,32,1024]{2,1,0:T(8,128)(2,1)}), bf16[8,32,1024]{2,1,0:T(8,128)(2,1)S(1)}, u32[]{:S(2)}, u32[]{:S(2)}) async-start(bf16[8,32,1024]{2,1,0:T(8,128)(2,1)} %reshape.81), calls=%async_computation.4 | async-start | bytes 1048576 | tf_op jit(solution)/shard_map/all_to_all | solution.py:18
  77.9 1.5 fusion.5
  79.5 8.1 %all-to-all-done.4 = bf16[8,32,1024]{2,1,0:T(8,128)(2,1)S(1)} async-done(((bf16[8,32,1024]{2,1,0:T(8,128)(2,1)}), bf16[8,32,1024]{2,1,0:T(8,128)(2,1)S(1)}, u32[]{:S(2)}, u32[]{:S(2)}) %all-to-all-start.4) | async-done | bytes 524320 | tf_op jit(solution)/shard_map/all_to_all | solution.py:18
  87.5 6.5 %all-to-all-start.1 = ((bf16[4,256,256]{2,1,0:T(8,128)(2,1)}), bf16[4,256,256]{2,1,0:T(8,128)(2,1)S(1)}, u32[]{:S(2)}, u32[]{:S(2)}) async-start(bf16[4,256,256]{2,1,0:T(8,128)(2,1)} %bitcast.80), calls=%async_computation.1 | async-start | bytes 1048576 | tf_op jit(solution)/shard_map/all_to_all | solution.py:18
  94.0 3.1 %copy.30 = bf16[4,8,256,128]{2,0,3,1:T(4,128)(2,1)S(1)} copy(bf16[4,8,256,128]{3,2,1,0:T(8,128)(2,1)} %bitcast.71) | data formatting | bytes 4194304 | tf_op jit(solution)/shard_map/reshape;squeeze | solution.py:50
  97.1 2.7 %reshape.78 = bf16[8,1024,128]{1,2,0:T(8,128)(2,1)} reshape(bf16[8,4,256,128]{2,1,3,0:T(4,128)(2,1)S(1)} %bitcast.67) | data formatting | bytes 4194304 | tf_op jit(solution)/shard_map/reshape | solution.py:51
  99.8 21.4 %all-to-all-done.1 = bf16[4,256,256]{2,1,0:T(8,128)(2,1)S(1)} async-done(((bf16[4,256,256]{2,1,0:T(8,128)(2,1)}), bf16[4,256,256]{2,1,0:T(8,128)(2,1)S(1)}, u32[]{:S(2)}, u32[]{:S(2)}) %all-to-all-start.1) | async-done | bytes 524320 | tf_op jit(solution)/shard_map/all_to_all | solution.py:18
  121.1 3.6 %all-to-all-start.2 = ((bf16[8,1024,128]{1,2,0:T(8,128)(2,1)}), bf16[8,1024,128]{1,2,0:T(8,128)(2,1)S(1)}, u32[]{:S(2)}, u32[]{:S(2)}) async-start(bf16[8,1024,128]{1,2,0:T(8,128)(2,1)} %reshape.78), calls=%async_computation.2 | async-start | bytes 4194304 | tf_op jit(solution)/shard_map/all_to_all | solution.py:18
  125.0 1.9 collective-permute-start
  127.5 29.1 %collective-permute-done = bf16[256,256]{1,0:T(8,128)(2,1)S(1)} collective-permute-done((bf16[256,256]{1,0:T(8,128)(2,1)S(1)}, bf16[256,256]{1,0:T(8,128)(2,1)S(1)}, u32[]{:S(2)}, u32[]{:S(2)}) %collective-permute-start) | collective-permute-done | bytes 131104 | tf_op jit(solution)/shard_map/ppermute | solution.py:62
  156.8 28.3 %all-gather = bf16[1088,256]{1,0:T(8,128)(2,1)S(1)} all-gather(bf16[272,256]{1,0:T(8,128)(2,1)S(1)} %maximum_maximum_fusion), channel_id=2, replica_groups=mesh['section'=16,'b'=4,'a'=8] {'b'}, dimensions={0}, use_global_device_ids=true | all-gather | bytes 696320 | tf_op jit(solution)/shard_map/all_gather | solution.py:68
  186.5 1.3 pad_maximum_fusion.1
  187.8 4.5 %all-to-all-start.5 = ((bf16[8,400,256]{2,1,0:T(8,128)(2,1)}), bf16[8,400,256]{2,1,0:T(8,128)(2,1)S(1)}, u32[]{:S(2)}, u32[]{:S(2)}) async-start(bf16[8,400,256]{2,1,0:T(8,128)(2,1)} %pad_maximum_fusion.1), calls=%async_computation.5 | async-start | bytes 3276800 | tf_op jit(solution)/shard_map/all_to_all | solution.py:18
  192.3 13.7 %all-to-all-done.5 = bf16[8,400,256]{2,1,0:T(8,128)(2,1)S(1)} async-done(((bf16[8,400,256]{2,1,0:T(8,128)(2,1)}), bf16[8,400,256]{2,1,0:T(8,128)(2,1)S(1)}, u32[]{:S(2)}, u32[]{:S(2)}) %all-to-all-start.5) | async-done | bytes 1638432 | tf_op jit(solution)/shard_map/all_to_all | solution.py:18
  207.0 0.9 fusion.10
  (39 shorter events, 3.8 us)
Async XLA Ops:
  0.0 39.9 %all-to-all-start.3 = ((bf16[4,8,8192]{2,1,0:T(8,128)(2,1)}), bf16[4,8,8192]{2,1,0:T(8,128)(2,1)S(1)}, u32[]{:S(2)}, u32[]{:S(2)}) async-start(bf16[4,8,8192]{2,1,0:T(8,128)(2,1)} %bitcast.79), calls=%async_computation.3 | async-start | bytes 1048576 | tf_op jit(solution)/shard_map/all_to_all | solution.py:18
  15.5 3.3 %copy-start.1 = (bf16[1,256,128]{2,1,0:T(8,128)(2,1)S(1)}, bf16[1,256,128]{2,1,0:T(8,128)(2,1)}, u32[]{:S(2)}) copy-start(bf16[1,256,128]{2,1,0:T(8,128)(2,1)} %param.6) | copy-start | bytes 196612
  39.9 34.4 %all-to-all-start = ((bf16[8,128,1280]{2,1,0:T(8,128)(2,1)}), bf16[8,128,1280]{2,1,0:T(8,128)(2,1)S(1)}, u32[]{:S(2)}, u32[]{:S(2)}) async-start(bf16[8,128,1280]{2,1,0:T(8,128)(2,1)} %pad_maximum_fusion), calls=%async_computation | async-start | bytes 5242880 | tf_op jit(solution)/shard_map/all_to_all | solution.py:18
  74.3 13.2 %all-to-all-start.4 = ((bf16[8,32,1024]{2,1,0:T(8,128)(2,1)}), bf16[8,32,1024]{2,1,0:T(8,128)(2,1)S(1)}, u32[]{:S(2)}, u32[]{:S(2)}) async-start(bf16[8,32,1024]{2,1,0:T(8,128)(2,1)} %reshape.81), calls=%async_computation.4 | async-start | bytes 1048576 | tf_op jit(solution)/shard_map/all_to_all | solution.py:18
  87.5 33.6 %all-to-all-start.1 = ((bf16[4,256,256]{2,1,0:T(8,128)(2,1)}), bf16[4,256,256]{2,1,0:T(8,128)(2,1)S(1)}, u32[]{:S(2)}, u32[]{:S(2)}) async-start(bf16[4,256,256]{2,1,0:T(8,128)(2,1)} %bitcast.80), calls=%async_computation.1 | async-start | bytes 1048576 | tf_op jit(solution)/shard_map/all_to_all | solution.py:18
  99.8 25.0 %copy-start = (bf16[1,256,256]{2,1,0:T(8,128)(2,1)S(1)}, bf16[1,256,256]{2,1,0:T(8,128)(2,1)}, u32[]{:S(2)}) copy-start(bf16[1,256,256]{2,1,0:T(8,128)(2,1)} %param.8) | copy-start | bytes 393220
  121.1 64.4 %all-to-all-start.2 = ((bf16[8,1024,128]{1,2,0:T(8,128)(2,1)}), bf16[8,1024,128]{1,2,0:T(8,128)(2,1)S(1)}, u32[]{:S(2)}, u32[]{:S(2)}) async-start(bf16[8,1024,128]{1,2,0:T(8,128)(2,1)} %reshape.78), calls=%async_computation.2 | async-start | bytes 4194304 | tf_op jit(solution)/shard_map/all_to_all | solution.py:18
  124.9 31.8 %copy-start.2 = (f32[1,256]{1,0:T(1,128)S(1)}, f32[1,256]{1,0:T(1,128)}, u32[]{:S(2)}) copy-start(f32[1,256]{1,0:T(1,128)} %param.9) | copy-start | bytes 3076
  125.0 31.6 %collective-permute-start = (bf16[256,256]{1,0:T(8,128)(2,1)S(1)}, bf16[256,256]{1,0:T(8,128)(2,1)S(1)}, u32[]{:S(2)}, u32[]{:S(2)}) collective-permute-start(bf16[256,256]{1,0:T(8,128)(2,1)S(1)} %fusion.15), channel_id=1, source_target_pairs={{0,32},{32,64},{64,96},{96,128},{128,160},{160,192},{192,224},{224... | collective-permute-start | bytes 393224 | tf_op jit(solution)/shard_map/ppermute | solution.py:62
  187.8 18.2 %all-to-all-start.5 = ((bf16[8,400,256]{2,1,0:T(8,128)(2,1)}), bf16[8,400,256]{2,1,0:T(8,128)(2,1)S(1)}, u32[]{:S(2)}, u32[]{:S(2)}) async-start(bf16[8,400,256]{2,1,0:T(8,128)(2,1)} %pad_maximum_fusion.1), calls=%async_computation.5 | async-start | bytes 3276800 | tf_op jit(solution)/shard_map/all_to_all | solution.py:18

commit v2 on v1

v2 whole, which is shorter than its diff:
```python
import jax
import jax.numpy as jnp
from jax import lax
from jax.experimental import pallas as pl
from jax.experimental.pallas import tpu as pltpu
from jax.sharding import Mesh, PartitionSpec as P

THETA = 500000.0
ROWS, COLS = 4, 8
BF16, F32 = jnp.bfloat16, jnp.float32
VMEM = pl.BlockSpec(memory_space=pltpu.VMEM)
SMEM = pl.BlockSpec(memory_space=pltpu.SMEM)
STATS = 16


def contract(lhs, rhs, lhs_dim, rhs_dim):
    return lax.dot_general(
        lhs, rhs, (((lhs_dim,), (rhs_dim,)), ((), ())), preferred_element_type=F32
    )


def exchange(pieces, axis):
    return lax.all_to_all(pieces, axis, 0, 0, tiled=True)


def turn(rows, cosine, sine):
    half = rows.shape[0] // 2
    first, second = rows[:half], rows[half:]
    return jnp.concatenate(
        [first * cosine - second * sine, second * cosine + first * sine], axis=0
    )


def stats_rows(total):
    high = total.astype(BF16).astype(F32)
    index = lax.broadcasted_iota(jnp.int32, (STATS, total.shape[1]), 0)
    low = jnp.where(index == 1, total - high, 0.0)
    return jnp.where(index == 0, high, low).astype(BF16)


def call(body, name, outs, in_specs, *operands):
    return pl.pallas_call(
        body,
        in_specs=in_specs,
        out_specs=jax.tree.map(lambda _: VMEM, outs),
        out_shape=outs,
        compiler_params=pltpu.CompilerParams(vmem_limit_bytes=40 * 2**20),
        name=name,
    )(*operands)


def out_pieces(out_weight, context):
    head, width = out_weight.shape[1:]
    tokens = context.shape[1]
    part = width // (ROWS * COLS)

    def body(*refs):
        strips, own, out = refs[:ROWS], refs[ROWS], refs[ROWS + 1]
        for r in range(ROWS):
            out[0, :, r * part:(r + 1) * part] = strips[r][0]
        out[0, :, ROWS * part:] = own[0].astype(F32).T.astype(BF16)

    def strip(r):
        return pl.BlockSpec((1, head, part), lambda a: (0, 0, r * COLS + a))

    return pl.pallas_call(
        body,
        grid=(COLS,),
        in_specs=[strip(r) for r in range(ROWS)]
        + [pl.BlockSpec((1, tokens, head), lambda a: (0, 0, 0))],
        out_specs=pl.BlockSpec((1, head, ROWS * part + tokens), lambda a: (a, 0, 0)),
        out_shape=jax.ShapeDtypeStruct((COLS, head, ROWS * part + tokens), BF16),
        name="out_pieces",
    )(*[out_weight] * ROWS, context)


def in_pieces(q_weight, kv_weight):
    width, head = q_weight.shape[1:]
    cols = kv_weight.shape[0]
    part = width // (ROWS * COLS)
    block = ROWS * part
    rows = block + cols * block // head

    def body(*refs):
        q_refs, kv_refs, out = refs[:ROWS], refs[ROWS:2 * ROWS], refs[2 * ROWS]
        for r in range(ROWS):
            out[0, r * part:(r + 1) * part] = q_refs[r][0]
            for k in range(part // head):
                at = block + (r * (part // head) + k) * cols
                out[0, at:at + cols] = kv_refs[r][:, k * head:(k + 1) * head]

    def q_strip(r):
        return pl.BlockSpec((1, part, head), lambda a: (0, r * COLS + a, 0))

    def kv_strip(r):
        return pl.BlockSpec((cols, part), lambda a: (0, r * COLS + a))

    return pl.pallas_call(
        body,
        grid=(COLS,),
        in_specs=[q_strip(r) for r in range(ROWS)] + [kv_strip(r) for r in range(ROWS)],
        out_specs=pl.BlockSpec((1, rows, head), lambda a: (a, 0, 0)),
        out_shape=jax.ShapeDtypeStruct((COLS, rows, head), BF16),
        name="in_pieces",
    )(*[q_weight] * ROWS, *[kv_weight] * ROWS)


def row_terms(got, residual, row):
    head = got.shape[1]
    tokens, part = residual.shape[1:]

    def body(row_ref, got_ref, residual_ref, *outs):
        context = got_ref[:, :, ROWS * part:].reshape(COLS * head, tokens)
        for k in range(ROWS):
            at = pl.multiple_of((row_ref[0] ^ k) * part, part)
            weight = got_ref[:, :, pl.ds(at, part)].reshape(COLS * head, part)
            terms = contract(weight, context, 0, 0)
            if k == 0:
                terms = terms + residual_ref[0].astype(F32).T
            outs[k][...] = terms.astype(BF16)

    outs = [jax.ShapeDtypeStruct((part, tokens), BF16)] * ROWS
    return call(body, "row_terms", outs, [SMEM, VMEM, VMEM], row, got, residual)


def scaled_sum(pieces, gain):
    part, tokens = pieces[0].shape

    def body(*refs):
        total = refs[0][...].astype(F32)
        for k in range(1, ROWS):
            total = total + refs[k][...].astype(F32)
        out = refs[ROWS + 1]
        out[:part] = (total * refs[ROWS][...]).astype(BF16)
        out[part:] = stats_rows(jnp.sum(total * total, axis=0, keepdims=True))

    outs = jax.ShapeDtypeStruct((part + STATS, tokens), BF16)
    return call(body, "scaled_sum", outs, [VMEM] * (ROWS + 1), *pieces, gain)


def projections(got, gathered, row):
    rows, head = got.shape[1:]
    tokens = gathered.shape[2]
    part = gathered.shape[1] - STATS
    block = ROWS * part
    chunks = block // head
    cols = (rows - block) // chunks
    each = cols // ROWS
    half = each // 2

    def body(row_ref, got_ref, gathered_ref, q_ref, *refs):
        kv_refs, stats_ref, scratch = refs[:ROWS], refs[ROWS], refs[ROWS + 1]
        features = gathered_ref[:, :part].reshape(block, tokens)
        for a in range(COLS):
            q_ref[a] = contract(got_ref[a, :block], features, 0, 0).astype(BF16)
        kv = jnp.zeros((COLS * cols, tokens), F32)
        for k in range(chunks):
            at = block + k * cols
            weight = got_ref[:, at:at + cols].reshape(COLS * cols, head)
            kv = kv + contract(weight, features[k * head:(k + 1) * head], 1, 0)
        size = COLS * cols
        to = lax.broadcasted_iota(jnp.int32, (size, size), 0)
        source = lax.broadcasted_iota(jnp.int32, (size, size), 1)
        group, rest = to // (COLS * each), to % (COLS * each)
        kind, rest = rest // (COLS * half), rest % (COLS * half)
        column, feature = rest // half, rest % half
        wanted = column * cols + group * each + kind * half + feature
        select = jnp.where(source == wanted, 1.0, 0.0).astype(BF16)
        scratch[...] = contract(select, kv.astype(BF16), 1, 0).astype(BF16)
        for k in range(ROWS):
            at = pl.multiple_of((row_ref[0] ^ k) * COLS * each, COLS * each)
            kv_refs[k][...] = scratch[pl.ds(at, COLS * each)]
        squares = gathered_ref[:, part:].astype(F32)
        squares = jnp.sum(jnp.sum(squares, axis=0), axis=0, keepdims=True)
        stats_ref[...] = stats_rows(squares)

    shapes = [(COLS, head, tokens)] + [(COLS * each, tokens)] * ROWS + [(STATS, tokens)]
    return pl.pallas_call(
        body,
        in_specs=[SMEM, VMEM, VMEM],
        out_specs=[VMEM] * len(shapes),
        out_shape=[jax.ShapeDtypeStruct(shape, BF16) for shape in shapes],
        scratch_shapes=[pltpu.VMEM((COLS * cols, tokens), BF16)],
        compiler_params=pltpu.CompilerParams(vmem_limit_bytes=40 * 2**20),
        name="projections",
    )(row, got, gathered)


def head_pieces(q_part, kv_parts, stats, row):
    head, tokens = q_part.shape[1:]
    share = head // ROWS

    def body(row_ref, q_ref, *refs):
        kv_refs, stats_ref, out = refs[:ROWS], refs[ROWS], refs[ROWS + 1]
        for a in range(COLS):
            out[a, :head] = q_ref[a]
            out[a, 3 * head:] = stats_ref[...]
            for k in range(ROWS):
                at = pl.multiple_of((row_ref[0] ^ k) * share, share)
                out[a, pl.ds(head + at, share)] = kv_refs[k][:share]
                out[a, pl.ds(2 * head + at, share)] = kv_refs[k][share:]

    outs = jax.ShapeDtypeStruct((COLS, 3 * head + STATS, tokens), BF16)
    specs = [SMEM] + [VMEM] * (ROWS + 2)
    return call(body, "head_pieces", outs, specs, row, q_part, *kv_parts, stats)


def on_device(context, out_weight, residual, gain, q_weight, kv_weight):
    tokens, head = context.shape[1:]
    width = out_weight.shape[2]
    row = lax.axis_index("b").reshape(1)
    sections = lax.axis_size("section")

    def to_row(piece, step, distance):
        route = [
            (s * ROWS + r, (s + distance) % sections * ROWS + (r ^ step))
            for s in range(sections)
            for r in range(ROWS)
        ]
        return lax.ppermute(piece, ("section", "b"), route)

    got = exchange(out_pieces(out_weight, context), "a")
    terms = row_terms(got, residual, row)

    pieces = in_pieces(q_weight, kv_weight[0].T)
    pieces, *terms = lax.optimization_barrier((pieces, *terms))
    weights = exchange(pieces, "a")

    received = [to_row(terms[k], k, 1) for k in range(ROWS)]
    gathered = lax.all_gather(scaled_sum(received, gain.T), "b", axis=0)
    q_part, *kv_parts, stats = projections(weights, gathered, row)
    kv_parts = [kv_parts[0]] + [to_row(kv_parts[k], k, 0) for k in range(1, ROWS)]
    summed = exchange(head_pieces(q_part, kv_parts, stats, row), "a")
    summed = jnp.sum(summed.astype(F32), axis=0)
    total = summed[3 * head] + summed[3 * head + 1]
    summed = summed[:3 * head] * lax.rsqrt(total / width + 1e-05)[None, :]

    positions = jnp.arange(tokens).astype(F32)
    frequency = THETA ** (-(jnp.arange(head // 2).astype(F32) * 2.0 / head))
    angles = frequency[:, None] * positions[None, :]
    cosine, sine = jnp.cos(angles), jnp.sin(angles)
    queries = turn(summed[:head], cosine, sine).astype(BF16)
    keys = summed[head:2 * head].astype(BF16).astype(F32)
    keys = turn(keys, cosine, sine).astype(BF16)
    values = summed[2 * head:].astype(BF16)
    scores = contract(queries, keys, 0, 0) * head ** (-0.5)
    order = jnp.arange(tokens)
    scores = jnp.where(order[:, None] >= order[None, :], scores, -1e30)
    softmax_weights = jax.nn.softmax(scores, axis=-1).astype(BF16)
    attended = contract(softmax_weights, values, 1, 1).astype(BF16)
    return attended[None]


def solution(mesh):
    sections = mesh.devices.shape[0]
    fine = Mesh(mesh.devices.reshape(sections, ROWS, COLS), ("section", "b", "a"))
    tensor = ("b", "a")
    placed = (
        P("section", None, tensor),
        P("section", tensor, None),
        P("section", None, tensor),
        P("section", tensor),
        P("section", None, tensor),
        P("section", None, tensor),
    )
    return jax.shard_map(
        on_device,
        mesh=fine,
        in_specs=placed,
        out_specs=P("section", None, tensor),
        check_vma=False,
    )
```

time: 210 us -> 182 us (0.87)
  waiting for transfers between devices: 120 us -> 84.9 us
  Pallas kernels: 0 us -> 16 us
  local copies, waits for them, and re-layouts: 15.9 us -> 0.14 us
  starting transfers between devices: 35.7 us -> 51.4 us
  other arithmetic: 4.22 us -> 0.7 us
  matrix products: 3.7 us -> 1.14 us
    all_to_all x6 -> x3, waiting for transfers between devices: 90.7 us -> 39.5 us  [exchange(): return lax.all_to_all(pieces, axis, 0, 0, tiled=True)]
    ppermute x1 -> x7, starting transfers between devices: 1.92 us -> 37.6 us  [to_row(): return lax.ppermute(piece, ('section', 'b'), route)]
    all_to_all x6 -> x3, starting transfers between devices: 33.8 us -> 13.8 us  [exchange(): return lax.all_to_all(pieces, axis, 0, 0, tiled=True)]
    ppermute x1 -> x7, waiting for transfers between devices: 29.1 us -> 45.5 us  [to_row(): return lax.ppermute(piece, ('section', 'b'), route)]
    pallas_call x0 -> x6, Pallas kernels: none -> 16 us  [the longest x1 6.12 us: out_pieces(): pl.pallas_call(body, grid=(COLS,), in_specs=[strip(r) for r in range(ROWS...]
    reshape x6 -> x0, local copies, waits for them, and re-layouts: 7.66 us -> none  [the longest x1 3.26 us: on_device(): out_cols = out_cols.reshape(COLS, head, block)]
    another operation x3 -> x0, local copies, waits for them, and re-layouts: 5.2 us -> none  [the longest x1 3.06 us: on_device(): q_rows = q_weight[0].reshape(ROWS, COLS, part, head).transpose(1, 0, 2, 3)]
    concatenate x4 -> x0, other arithmetic: 3.22 us -> none  [the longest x1 1.73 us: on_device(): got = exchange(jnp.concatenate([out_cols, own], axis=2), 'a')]
  transfers between devices with their start and end apart: 7 -> 10, of which waited for: 6 -> 6; matrix products, arithmetic and copies ran while one was open for 9% -> 0% of each run, Pallas kernels for 0% -> 3%
where the time goes in v2:
time: 182 us; the launch traced here: 181 us
  waiting for transfers between devices  84.9 us (47%)
  starting transfers between devices  51.4 us (28%)
  blocking collectives  26.7 us (15%)
  Pallas kernels  16 us (9%)
    ppermute x7, waiting for transfers between devices, to_row(): return lax.ppermute(piece, ('section', 'b'), route)  45.5 us
    all_to_all x3, waiting for transfers between devices, exchange(): return lax.all_to_all(pieces, axis, 0, 0, tiled=True)  39.5 us
    ppermute x7, starting transfers between devices, to_row(): return lax.ppermute(piece, ('section', 'b'), route)  37.6 us
    all_gather x1, blocking collectives, on_device(): gathered = lax.all_gather(scaled_sum(received, gain.T), 'b', axis=0)  26.7 us
    all_to_all x3, starting transfers between devices, exchange(): return lax.all_to_all(pieces, axis, 0, 0, tiled=True)  13.8 us
    pallas_call x1, Pallas kernels, out_pieces(): pl.pallas_call(body, grid=(COLS,), in_specs=[strip(r) for r in range(ROWS...  6.12 us
    pallas_call x1, Pallas kernels, in_pieces(): pl.pallas_call(body, grid=(COLS,), in_specs=[q_strip(r) for r in range(RO...  5.93 us
  transfers between devices with their start and end apart: 10, of which 6 were waited for; matrix products, arithmetic and copies ran while one was open for 0% of the time, Pallas kernels for 3%

profile of v2, /device:TPU:6, one launch (start us, length us, event | category | flops | bytes accessed | tf_op | source)
XLA Modules:
  0.0 181.2 jit_solution(5135147345180225841)
XLA Ops:
  0.0 6.1 %out_pieces.1 = bf16[8,128,1280]{2,1,0:T(8,128)(2,1)} custom-call(bf16[1,128,8192]{2,1,0:T(8,128)(2,1)} %refs_3_.3, bf16[1,128,8192]{2,1,0:T(8,128)(2,1)} %refs_3_.3, bf16[1,128,8192]{2,1,0:T(8,128)(2,1)} %refs_3_.3, bf16[1,128,8192]{2,1,0:T(8,128)(2,1)} %refs_3_.3, bf16[1,256,128]{2,1,0:T(8,128)(2,1)} %refs_4_.1), custom_call_target="tpu_custom_call" | custom-call | tf_op jit(solution)/shard_map/out_pieces/pallas_call | solution.py:66
  6.1 5.8 %all-to-all-start = ((bf16[8,128,1280]{2,1,0:T(8,128)(2,1)}), bf16[8,128,1280]{2,1,0:T(8,128)(2,1)S(1)}, u32[]{:S(2)}, u32[]{:S(2)}) async-start(bf16[8,128,1280]{2,1,0:T(8,128)(2,1)} %out_pieces.1), calls=%async_computation | async-start | bytes 5242880 | tf_op jit(solution)/shard_map/all_to_all | solution.py:23
  12.0 5.9 %in_pieces.1 = bf16[8,1280,128]{2,1,0:T(8,128)(2,1)} custom-call(bf16[1,8192,128]{2,1,0:T(8,128)(2,1)} %refs_3_.2, bf16[1,8192,128]{2,1,0:T(8,128)(2,1)} %refs_3_.2, bf16[1,8192,128]{2,1,0:T(8,128)(2,1)} %refs_3_.2, bf16[1,8192,128]{2,1,0:T(8,128)(2,1)} %refs_3_.2, bf16[32,8192]{1,0:T(8,128)(2,1)} %bitcast.10, bf16[32,8192]{1,0:T(8,128)(2,1)} %bitcast.11, ...), custom_call_target="tpu_custom_call" | custom-call | tf_op jit(solution)/shard_map/in_pieces/pallas_call | solution.py:98
  17.9 25.7 %all-to-all-done.got_ref = bf16[8,128,1280]{2,1,0:T(8,128)(2,1)S(1)} async-done(((bf16[8,128,1280]{2,1,0:T(8,128)(2,1)}), bf16[8,128,1280]{2,1,0:T(8,128)(2,1)S(1)}, u32[]{:S(2)}, u32[]{:S(2)}) %all-to-all-start) | async-done | bytes 2621472 | tf_op jit(solution)/shard_map/all_to_all | solution.py:23
  43.6 1.3 row_terms.1
  45.0 3.8 %all-to-all-start.1 = ((bf16[8,1280,128]{2,1,0:T(8,128)(2,1)}), bf16[8,1280,128]{2,1,0:T(8,128)(2,1)S(1)}, u32[]{:S(2)}, u32[]{:S(2)}) async-start(bf16[8,1280,128]{2,1,0:T(8,128)(2,1)} %in_pieces.1), calls=%async_computation.1 | async-start | bytes 5242880 | tf_op jit(solution)/shard_map/all_to_all | solution.py:23
  48.7 1.9 %collective-permute-start = (bf16[256,256]{1,0:T(8,128)(2,1)}, bf16[256,256]{1,0:T(8,128)(2,1)S(1)}, u32[]{:S(2)}, u32[]{:S(2)}) collective-permute-start(bf16[256,256]{1,0:T(8,128)(2,1)} %get-tuple-element.25), channel_id=1, source_target_pairs={{0,32},{8,40},{16,48},{24,56},{32,64},{40,72},{48,80},{56,88},{64,... | collective-permute-start | bytes 393224 | tf_op jit(solution)/shard_map/ppermute | solution.py:220
  50.6 16.0 %collective-permute-start.1 = (bf16[256,256]{1,0:T(8,128)(2,1)}, bf16[256,256]{1,0:T(8,128)(2,1)S(1)}, u32[]{:S(2)}, u32[]{:S(2)}) collective-permute-start(bf16[256,256]{1,0:T(8,128)(2,1)} %get-tuple-element.26), channel_id=1, source_target_pairs={{0,40},{8,32},{16,56},{24,48},{32,72},{40,64},{48,88},{56,80},{64,... | collective-permute-start | bytes 393224 | tf_op jit(solution)/shard_map/ppermute | solution.py:220
  66.7 2.8 %collective-permute-start.2 = (bf16[256,256]{1,0:T(8,128)(2,1)S(1)}, bf16[256,256]{1,0:T(8,128)(2,1)S(1)}, u32[]{:S(2)}, u32[]{:S(2)}) collective-permute-start(bf16[256,256]{1,0:T(8,128)(2,1)S(1)} %get-tuple-element.27), channel_id=1, source_target_pairs={{0,48},{8,56},{16,32},{24,40},{32,80},{40,88},{48,64},{56,72},{64,... | collective-permute-start | bytes 393224 | tf_op jit(solution)/shard_map/ppermute | solution.py:220
  69.5 2.8 %collective-permute-start.3 = (bf16[256,256]{1,0:T(8,128)(2,1)S(1)}, bf16[256,256]{1,0:T(8,128)(2,1)S(1)}, u32[]{:S(2)}, u32[]{:S(2)}) collective-permute-start(bf16[256,256]{1,0:T(8,128)(2,1)S(1)} %get-tuple-element.28), channel_id=1, source_target_pairs={{0,56},{8,48},{16,40},{24,32},{32,88},{40,80},{48,72},{56,64},{64,... | collective-permute-start | bytes 393224 | tf_op jit(solution)/shard_map/ppermute | solution.py:220
  72.5 32.5 %collective-permute-done.refs_0_ = bf16[256,256]{1,0:T(8,128)(2,1)S(1)} collective-permute-done((bf16[256,256]{1,0:T(8,128)(2,1)}, bf16[256,256]{1,0:T(8,128)(2,1)S(1)}, u32[]{:S(2)}, u32[]{:S(2)}) %collective-permute-start) | collective-permute-done | bytes 131104 | tf_op jit(solution)/shard_map/ppermute | solution.py:220
  105.0 3.7 %collective-permute-done.1.refs_1_ = bf16[256,256]{1,0:T(8,128)(2,1)S(1)} collective-permute-done((bf16[256,256]{1,0:T(8,128)(2,1)}, bf16[256,256]{1,0:T(8,128)(2,1)S(1)}, u32[]{:S(2)}, u32[]{:S(2)}) %collective-permute-start.1) | collective-permute-done | bytes 131104 | tf_op jit(solution)/shard_map/ppermute | solution.py:220
  108.7 0.9 collective-permute-done.3.refs_3_
  109.7 26.7 %all-gather = bf16[1088,256]{1,0:T(8,128)(2,1)S(1)} all-gather(bf16[272,256]{1,0:T(8,128)(2,1)S(1)} %scaled_sum.1), channel_id=2, replica_groups=mesh['section'=16,'b'=4,'a'=8] {'b'}, dimensions={0}, use_global_device_ids=true | all-gather | bytes 696320 | tf_op jit(solution)/shard_map/all_gather | solution.py:230
  136.4 1.2 projections.1
  137.6 3.3 %collective-permute-start.4 = (bf16[64,256]{1,0:T(8,128)(2,1)S(1)}, bf16[64,256]{1,0:T(8,128)(2,1)S(1)}, u32[]{:S(2)}, u32[]{:S(2)}) collective-permute-start(bf16[64,256]{1,0:T(8,128)(2,1)S(1)} %get-tuple-element.31), channel_id=1, source_target_pairs={{0,8},{8,0},{16,24},{24,16},{32,40},{40,32},{48,56},{56,48},{64,72... | collective-permute-start | bytes 98312 | tf_op jit(solution)/shard_map/ppermute | solution.py:220
  141.0 7.5 %collective-permute-start.5 = (bf16[64,256]{1,0:T(8,128)(2,1)S(1)}, bf16[64,256]{1,0:T(8,128)(2,1)S(1)}, u32[]{:S(2)}, u32[]{:S(2)}) collective-permute-start(bf16[64,256]{1,0:T(8,128)(2,1)S(1)} %get-tuple-element.32), channel_id=1, source_target_pairs={{0,16},{8,24},{16,0},{24,8},{32,48},{40,56},{48,32},{56,40},{64,80... | collective-permute-start | bytes 98312 | tf_op jit(solution)/shard_map/ppermute | solution.py:220
  148.4 3.2 %collective-permute-start.6 = (bf16[64,256]{1,0:T(8,128)(2,1)S(1)}, bf16[64,256]{1,0:T(8,128)(2,1)S(1)}, u32[]{:S(2)}, u32[]{:S(2)}) collective-permute-start(bf16[64,256]{1,0:T(8,128)(2,1)S(1)} %get-tuple-element.33), channel_id=1, source_target_pairs={{0,24},{8,16},{16,8},{24,0},{32,56},{40,48},{48,40},{56,32},{64,88... | collective-permute-start | bytes 98312 | tf_op jit(solution)/shard_map/ppermute | solution.py:220
  151.7 8.4 %collective-permute-done.6.refs_3_ = bf16[64,256]{1,0:T(8,128)(2,1)S(1)} collective-permute-done((bf16[64,256]{1,0:T(8,128)(2,1)S(1)}, bf16[64,256]{1,0:T(8,128)(2,1)S(1)}, u32[]{:S(2)}, u32[]{:S(2)}) %collective-permute-start.6) | collective-permute-done | bytes 32800 | tf_op jit(solution)/shard_map/ppermute | solution.py:220
  160.1 1.3 head_pieces.1
  161.4 4.2 %all-to-all-start.2 = ((bf16[8,400,256]{2,1,0:T(8,128)(2,1)}), bf16[8,400,256]{2,1,0:T(8,128)(2,1)S(1)}, u32[]{:S(2)}, u32[]{:S(2)}) async-start(bf16[8,400,256]{2,1,0:T(8,128)(2,1)} %head_pieces.1), calls=%async_computation.2 | async-start | bytes 3276800 | tf_op jit(solution)/shard_map/all_to_all | solution.py:23
  165.6 13.7 %all-to-all-done.2 = bf16[8,400,256]{2,1,0:T(8,128)(2,1)S(1)} async-done(((bf16[8,400,256]{2,1,0:T(8,128)(2,1)}), bf16[8,400,256]{2,1,0:T(8,128)(2,1)S(1)}, u32[]{:S(2)}, u32[]{:S(2)}) %all-to-all-start.2) | async-done | bytes 1638432 | tf_op jit(solution)/shard_map/all_to_all | solution.py:23
  179.7 0.3 fusion.16
  180.3 0.9 fusion.1
  (18 shorter events, 0.9 us)
Async XLA Ops:
  6.1 37.5 %all-to-all-start = ((bf16[8,128,1280]{2,1,0:T(8,128)(2,1)}), bf16[8,128,1280]{2,1,0:T(8,128)(2,1)S(1)}, u32[]{:S(2)}, u32[]{:S(2)}) async-start(bf16[8,128,1280]{2,1,0:T(8,128)(2,1)} %out_pieces.1), calls=%async_computation | async-start | bytes 5242880 | tf_op jit(solution)/shard_map/all_to_all | solution.py:23
  11.9 31.7 %copy-start = (bf16[1,256,256]{2,1,0:T(8,128)(2,1)S(1)}, bf16[1,256,256]{2,1,0:T(8,128)(2,1)}, u32[]{:S(2)}) copy-start(bf16[1,256,256]{2,1,0:T(8,128)(2,1)} %residual_ref.1) | copy-start | bytes 393220
  44.9 27.4 %copy-start.1 = (f32[1,256]{1,0:T(1,128)S(1)}, f32[1,256]{1,0:T(1,128)}, u32[]{:S(2)}) copy-start(f32[1,256]{1,0:T(1,128)} %param.9) | copy-start | bytes 3076
  45.0 91.4 %all-to-all-start.1 = ((bf16[8,1280,128]{2,1,0:T(8,128)(2,1)}), bf16[8,1280,128]{2,1,0:T(8,128)(2,1)S(1)}, u32[]{:S(2)}, u32[]{:S(2)}) async-start(bf16[8,1280,128]{2,1,0:T(8,128)(2,1)} %in_pieces.1), calls=%async_computation.1 | async-start | bytes 5242880 | tf_op jit(solution)/shard_map/all_to_all | solution.py:23
  48.7 56.3 %collective-permute-start = (bf16[256,256]{1,0:T(8,128)(2,1)}, bf16[256,256]{1,0:T(8,128)(2,1)S(1)}, u32[]{:S(2)}, u32[]{:S(2)}) collective-permute-start(bf16[256,256]{1,0:T(8,128)(2,1)} %get-tuple-element.25), channel_id=1, source_target_pairs={{0,32},{8,40},{16,48},{24,56},{32,64},{40,72},{48,80},{56,88},{64,... | collective-permute-start | bytes 393224 | tf_op jit(solution)/shard_map/ppermute | solution.py:220
  50.6 58.1 %collective-permute-start.1 = (bf16[256,256]{1,0:T(8,128)(2,1)}, bf16[256,256]{1,0:T(8,128)(2,1)S(1)}, u32[]{:S(2)}, u32[]{:S(2)}) collective-permute-start(bf16[256,256]{1,0:T(8,128)(2,1)} %get-tuple-element.26), channel_id=1, source_target_pairs={{0,40},{8,32},{16,56},{24,48},{32,72},{40,64},{48,88},{56,80},{64,... | collective-permute-start | bytes 393224 | tf_op jit(solution)/shard_map/ppermute | solution.py:220
  66.7 42.0 %collective-permute-start.2 = (bf16[256,256]{1,0:T(8,128)(2,1)S(1)}, bf16[256,256]{1,0:T(8,128)(2,1)S(1)}, u32[]{:S(2)}, u32[]{:S(2)}) collective-permute-start(bf16[256,256]{1,0:T(8,128)(2,1)S(1)} %get-tuple-element.27), channel_id=1, source_target_pairs={{0,48},{8,56},{16,32},{24,40},{32,80},{40,88},{48,64},{56,72},{64,... | collective-permute-start | bytes 393224 | tf_op jit(solution)/shard_map/ppermute | solution.py:220
  69.5 40.1 %collective-permute-start.3 = (bf16[256,256]{1,0:T(8,128)(2,1)S(1)}, bf16[256,256]{1,0:T(8,128)(2,1)S(1)}, u32[]{:S(2)}, u32[]{:S(2)}) collective-permute-start(bf16[256,256]{1,0:T(8,128)(2,1)S(1)} %get-tuple-element.28), channel_id=1, source_target_pairs={{0,56},{8,48},{16,40},{24,32},{32,88},{40,80},{48,72},{56,64},{64,... | collective-permute-start | bytes 393224 | tf_op jit(solution)/shard_map/ppermute | solution.py:220
  137.6 14.0 %collective-permute-start.4 = (bf16[64,256]{1,0:T(8,128)(2,1)S(1)}, bf16[64,256]{1,0:T(8,128)(2,1)S(1)}, u32[]{:S(2)}, u32[]{:S(2)}) collective-permute-start(bf16[64,256]{1,0:T(8,128)(2,1)S(1)} %get-tuple-element.31), channel_id=1, source_target_pairs={{0,8},{8,0},{16,24},{24,16},{32,40},{40,32},{48,56},{56,48},{64,72... | collective-permute-start | bytes 98312 | tf_op jit(solution)/shard_map/ppermute | solution.py:220
  141.0 10.7 %collective-permute-start.5 = (bf16[64,256]{1,0:T(8,128)(2,1)S(1)}, bf16[64,256]{1,0:T(8,128)(2,1)S(1)}, u32[]{:S(2)}, u32[]{:S(2)}) collective-permute-start(bf16[64,256]{1,0:T(8,128)(2,1)S(1)} %get-tuple-element.32), channel_id=1, source_target_pairs={{0,16},{8,24},{16,0},{24,8},{32,48},{40,56},{48,32},{56,40},{64,80... | collective-permute-start | bytes 98312 | tf_op jit(solution)/shard_map/ppermute | solution.py:220
  148.4 11.6 %collective-permute-start.6 = (bf16[64,256]{1,0:T(8,128)(2,1)S(1)}, bf16[64,256]{1,0:T(8,128)(2,1)S(1)}, u32[]{:S(2)}, u32[]{:S(2)}) collective-permute-start(bf16[64,256]{1,0:T(8,128)(2,1)S(1)} %get-tuple-element.33), channel_id=1, source_target_pairs={{0,24},{8,16},{16,8},{24,0},{32,56},{40,48},{48,40},{56,32},{64,88... | collective-permute-start | bytes 98312 | tf_op jit(solution)/shard_map/ppermute | solution.py:220
  161.4 18.0 %all-to-all-start.2 = ((bf16[8,400,256]{2,1,0:T(8,128)(2,1)}), bf16[8,400,256]{2,1,0:T(8,128)(2,1)S(1)}, u32[]{:S(2)}, u32[]{:S(2)}) async-start(bf16[8,400,256]{2,1,0:T(8,128)(2,1)} %head_pieces.1), calls=%async_computation.2 | async-start | bytes 3276800 | tf_op jit(solution)/shard_map/all_to_all | solution.py:23

commit v3 on v2

v3 whole, which is shorter than its diff:
```python
import jax
import jax.numpy as jnp
from jax import lax
from jax.experimental import pallas as pl
from jax.experimental.pallas import tpu as pltpu
from jax.sharding import Mesh, PartitionSpec as P

THETA = 500000.0
ROWS, PAIR, LINE = 4, 2, 4
COLS = PAIR * LINE
BF16, F32 = jnp.bfloat16, jnp.float32
VMEM = pl.BlockSpec(memory_space=pltpu.VMEM)
SMEM = pl.BlockSpec(memory_space=pltpu.SMEM)
STATS = 16


def contract(lhs, rhs, lhs_dim, rhs_dim):
    return lax.dot_general(
        lhs, rhs, (((lhs_dim,), (rhs_dim,)), ((), ())), preferred_element_type=F32
    )


def exchange(pieces, axis):
    return lax.all_to_all(pieces, axis, 0, 0, tiled=True)


def turn(rows, cosine, sine):
    half = rows.shape[0] // 2
    first, second = rows[:half], rows[half:]
    return jnp.concatenate(
        [first * cosine - second * sine, second * cosine + first * sine], axis=0
    )


def stats_rows(total):
    high = total.astype(BF16).astype(F32)
    index = lax.broadcasted_iota(jnp.int32, (STATS, total.shape[1]), 0)
    low = jnp.where(index == 1, total - high, 0.0)
    return jnp.where(index == 0, high, low).astype(BF16)


def call(body, name, outs, in_specs, *operands):
    return pl.pallas_call(
        body,
        in_specs=in_specs,
        out_specs=jax.tree.map(lambda _: VMEM, outs),
        out_shape=outs,
        compiler_params=pltpu.CompilerParams(vmem_limit_bytes=40 * 2**20),
        name=name,
    )(*operands)


def out_pieces(out_weight, context):
    head, width = out_weight.shape[1:]
    tokens = context.shape[1]
    part = width // (ROWS * COLS)
    block = ROWS * part

    def body(weight, own, out, staged, sems, out_sems):
        def strip(a, r):
            return pltpu.make_async_copy(
                weight.at[0, :, pl.ds((r * COLS + a) * part, part)],
                staged.at[a, :, pl.ds(r * part, part)],
                sems.at[a, r],
            )

        for a in range(COLS):
            for r in range(ROWS):
                strip(a, r).start()
        turned = own[0].astype(F32).T.astype(BF16)
        for a in range(COLS):
            staged[a, :, block:] = turned
        outs = [pltpu.make_async_copy(staged.at[a], out.at[a], out_sems.at[a]) for a in range(COLS)]
        for a in range(COLS):
            for r in range(ROWS):
                strip(a, r).wait()
            outs[a].start()
        for copy in outs:
            copy.wait()

    shape = (COLS, head, block + tokens)
    return pl.pallas_call(
        body,
        in_specs=[pl.BlockSpec(memory_space=pl.ANY), VMEM],
        out_specs=pl.BlockSpec(memory_space=pl.ANY),
        out_shape=jax.ShapeDtypeStruct(shape, BF16),
        scratch_shapes=[
            pltpu.VMEM(shape, BF16),
            pltpu.SemaphoreType.DMA((COLS, ROWS)),
            pltpu.SemaphoreType.DMA((COLS,)),
        ],
        compiler_params=pltpu.CompilerParams(vmem_limit_bytes=40 * 2**20),
        name="out_pieces",
    )(out_weight, context)


def in_pieces(q_weight, kv_weight, side):
    width, head = q_weight.shape[1:]
    cols = kv_weight.shape[0]
    part = width // (ROWS * COLS)
    strips = ROWS * PAIR
    block = strips * part
    rows = block + cols * block // head

    def body(side_ref, *refs):
        q_refs, kv_refs, out = refs[:strips], refs[strips:2 * strips], refs[2 * strips]
        for r in range(strips):
            out[0, r * part:(r + 1) * part] = q_refs[r][0]
            for k in range(part // head):
                at = block + (r * (part // head) + k) * cols
                out[0, at:at + cols] = kv_refs[r][:, k * head:(k + 1) * head]

    def place(r, y, side_ref):
        return r % ROWS * COLS + (side_ref[0] ^ (r // ROWS)) * LINE + y

    def q_strip(r):
        return pl.BlockSpec((1, part, head), lambda y, s: (0, place(r, y, s), 0))

    def kv_strip(r):
        return pl.BlockSpec((cols, part), lambda y, s: (0, place(r, y, s)))

    return pl.pallas_call(
        body,
        grid_spec=pltpu.PrefetchScalarGridSpec(
            num_scalar_prefetch=1,
            grid=(LINE,),
            in_specs=[q_strip(r) for r in range(strips)]
            + [kv_strip(r) for r in range(strips)],
            out_specs=pl.BlockSpec((1, rows, head), lambda y, s: (y, 0, 0)),
        ),
        out_shape=jax.ShapeDtypeStruct((LINE, rows, head), BF16),
        name="in_pieces",
    )(side, *[q_weight] * strips, *[kv_weight] * strips)


def row_terms(got, residual, row):
    head = got.shape[1]
    tokens, part = residual.shape[1:]

    def body(row_ref, got_ref, residual_ref, *outs):
        context = got_ref[:, :, ROWS * part:].reshape(COLS * head, tokens)
        for k in range(ROWS):
            at = pl.multiple_of((row_ref[0] ^ k) * part, part)
            weight = got_ref[:, :, pl.ds(at, part)].reshape(COLS * head, part)
            terms = contract(weight, context, 0, 0)
            if k == 0:
                terms = terms + residual_ref[0].astype(F32).T
            outs[k][...] = terms.astype(BF16)

    outs = [jax.ShapeDtypeStruct((part, tokens), BF16)] * ROWS
    return call(body, "row_terms", outs, [SMEM, VMEM, VMEM], row, got, residual)


def scaled_sum(pieces, gain):
    part, tokens = pieces[0].shape

    def body(*refs):
        total = refs[0][...].astype(F32)
        for k in range(1, ROWS):
            total = total + refs[k][...].astype(F32)
        out = refs[ROWS + 1]
        out[:part] = (total * refs[ROWS][...]).astype(BF16)
        out[part:] = stats_rows(jnp.sum(total * total, axis=0, keepdims=True))

    outs = jax.ShapeDtypeStruct((part + STATS, tokens), BF16)
    return call(body, "scaled_sum", outs, [VMEM] * (ROWS + 1), *pieces, gain)


def projections(got, own, other):
    rows, head = got.shape[1:]
    tokens = own.shape[2]
    part = own.shape[1] - STATS
    half = ROWS * part
    block = PAIR * half
    chunks = block // head
    cols = (rows - block) // chunks
    each = cols // ROWS
    size = LINE * cols

    def body(got_ref, own_ref, other_ref, out):
        sides = [ref[:, :part].reshape(half, tokens) for ref in (own_ref, other_ref)]
        features = jnp.concatenate(sides, axis=0)
        kv = jnp.zeros((size, tokens), F32)
        for k in range(chunks):
            at = block + k * cols
            weight = got_ref[:, at:at + cols].reshape(size, head)
            kv = kv + contract(weight, features[k * head:(k + 1) * head], 1, 0)
        to = lax.broadcasted_iota(jnp.int32, (size, size), 0)
        source = lax.broadcasted_iota(jnp.int32, (size, size), 1)
        group, rest = to // (LINE * each), to % (LINE * each)
        kind, rest = rest // (LINE * each // 2), rest % (LINE * each // 2)
        column, feature = rest // (each // 2), rest % (each // 2)
        wanted = column * cols + group * each + kind * (each // 2) + feature
        select = jnp.where(source == wanted, 1.0, 0.0).astype(BF16)
        kv = contract(select, kv.astype(BF16), 1, 0).astype(BF16)
        squares = own_ref[:, part:].astype(F32) + other_ref[:, part:].astype(F32)
        squares = jnp.sum(jnp.sum(squares, axis=0), axis=0, keepdims=True)
        stats = stats_rows(squares)
        for y in range(LINE):
            out[y, :head] = contract(got_ref[y, :block], features, 0, 0).astype(BF16)
            out[y, head:head + size] = kv
            out[y, head + size:] = stats

    outs = jax.ShapeDtypeStruct((LINE, head + size + STATS, tokens), BF16)
    return call(body, "projections", outs, [VMEM] * 3, got, own, other)


def head_inputs(got, cosine, sine, width):
    line, rows, tokens = got.shape
    head = 2 * cosine.shape[0]
    share = (rows - head - STATS) // ROWS

    def body(got_ref, cosine_ref, sine_ref, q_ref, kv_ref):
        total = got_ref[0].astype(F32)
        for y in range(1, line):
            total = total + got_ref[y].astype(F32)
        squares = jnp.sum(total[rows - STATS:], axis=0, keepdims=True)
        total = total[:rows - STATS] * lax.rsqrt(squares / width + 1e-05)
        q_ref[...] = turn(total[:head], cosine_ref[...], sine_ref[...]).astype(BF16)
        for r in range(ROWS):
            at = head + r * share
            for z in range(PAIR):
                kv_ref[r * PAIR + z] = total[at:at + share].astype(BF16)

    outs = [
        jax.ShapeDtypeStruct((head, tokens), BF16),
        jax.ShapeDtypeStruct((ROWS * PAIR, share, tokens), BF16),
    ]
    return call(body, "head_inputs", outs, [VMEM] * 3, got, cosine, sine)


def attention(queries, pairs, cosine, sine):
    head, tokens = queries.shape
    groups, share = pairs.shape[:2]

    def body(q_ref, pairs_ref, cosine_ref, sine_ref, out):
        keys = pairs_ref[:, :share // 2].reshape(head, tokens).astype(F32)
        values = pairs_ref[:, share // 2:].reshape(head, tokens)
        keys = turn(keys, cosine_ref[...], sine_ref[...]).astype(BF16)
        scores = contract(q_ref[...], keys, 0, 0) * head ** (-0.5)
        at = lax.broadcasted_iota(jnp.int32, (tokens, tokens), 0)
        key_at = lax.broadcasted_iota(jnp.int32, (tokens, tokens), 1)
        scores = jnp.where(at >= key_at, scores, -1e30)
        weights = jnp.exp(scores - jnp.max(scores, axis=1, keepdims=True))
        weights = weights / jnp.sum(weights, axis=1, keepdims=True)
        out[0] = contract(weights.astype(BF16), values, 1, 1).astype(BF16)

    outs = jax.ShapeDtypeStruct((1, tokens, head), BF16)
    return call(body, "attention", outs, [VMEM] * 4, queries, pairs, cosine, sine)


def on_device(context, out_weight, residual, gain, q_weight, kv_weight):
    tokens, head = context.shape[1:]
    width = out_weight.shape[2]
    row = lax.axis_index("b").reshape(1)
    sections = lax.axis_size("section")

    def to_row(piece, step, distance):
        route = [
            (s * ROWS + r, (s + distance) % sections * ROWS + (r ^ step))
            for s in range(sections)
            for r in range(ROWS)
        ]
        return lax.ppermute(piece, ("section", "b"), route)

    got = exchange(out_pieces(out_weight, context), ("z", "y"))
    terms = row_terms(got, residual, row)

    pieces = in_pieces(q_weight, kv_weight[0].T, lax.axis_index("z").reshape(1))
    pieces, *terms = lax.optimization_barrier((pieces, *terms))
    weights = exchange(pieces, "y")

    positions = jnp.arange(tokens).astype(F32)
    frequency = THETA ** (-(jnp.arange(head // 2).astype(F32) * 2.0 / head))
    angles = frequency[:, None] * positions[None, :]
    cosine, sine = jnp.cos(angles), jnp.sin(angles)

    received = [to_row(terms[k], k, 1) for k in range(ROWS)]
    gathered = lax.all_gather(scaled_sum(received, gain.T), "b", axis=0)
    other = lax.ppermute(gathered, "z", [(0, 1), (1, 0)])
    summed = exchange(projections(weights, gathered, other), "y")
    queries, pairs = head_inputs(summed, cosine, sine, width)
    return attention(queries, exchange(pairs, ("b", "z")), cosine, sine)


def solution(mesh):
    sections = mesh.devices.shape[0]
    fine = Mesh(mesh.devices.reshape(sections, ROWS, PAIR, LINE), ("section", "b", "z", "y"))
    tensor = ("b", "z", "y")
    placed = (
        P("section", None, tensor),
        P("section", tensor, None),
        P("section", None, tensor),
        P("section", tensor),
        P("section", None, tensor),
        P("section", None, tensor),
    )
    return jax.shard_map(
        on_device,
        mesh=fine,
        in_specs=placed,
        out_specs=P("section", None, tensor),
        check_vma=False,
    )
```

time: 182 us -> 169 us (0.929)
  waiting for transfers between devices: 84.9 us -> 64.1 us
  blocking collectives: 26.7 us -> 44.5 us
  starting transfers between devices: 51.4 us -> 42.2 us
  local copies, waits for them, and re-layouts: 0.14 us -> 6.75 us
  Pallas kernels: 16 us -> 10.2 us
    ppermute x7 -> x4, waiting for transfers between devices: 45.5 us -> 13.9 us  [to_row(): return lax.ppermute(piece, ('section', 'b'), route)]
    all_to_all x0 -> x1, blocking collectives: none -> 17.6 us  [exchange(): return lax.all_to_all(pieces, axis, 0, 0, tiled=True)]
    ppermute x7 -> x4, starting transfers between devices: 37.6 us -> 23.6 us  [to_row(): return lax.ppermute(piece, ('section', 'b'), route)]
    ppermute x0 -> x1, waiting for transfers between devices: none -> 13 us  [on_device(): other = lax.ppermute(gathered, 'z', [(0, 1), (1, 0)])]
    pallas_call x3 -> x2, Pallas kernels: 13.3 us -> 5.85 us  [the longest x1 4.22 us: in_pieces(): pl.pallas_call(body, grid_spec=pltpu.PrefetchScalarGridSpec(num_scalar_pr...]
    unnamed x4 -> x16, local copies, waits for them, and re-layouts: 0.01 us -> 6.62 us
    ppermute x0 -> x1, starting transfers between devices: none -> 5.11 us  [on_device(): other = lax.ppermute(gathered, 'z', [(0, 1), (1, 0)])]
    all_to_all x3, waiting for transfers between devices: 39.5 us -> 37.2 us  [exchange(): return lax.all_to_all(pieces, axis, 0, 0, tiled=True)]
  transfers between devices with their start and end apart: 10 -> 8, of which waited for: 6 -> 6; matrix products, arithmetic and copies ran while one was open for 0% -> 0% of each run, Pallas kernels for 3% -> 3%
where the time goes in v3:
time: 169 us; the launch traced here: 168 us
  waiting for transfers between devices  64.1 us (38%)
  blocking collectives  44.5 us (26%)
  starting transfers between devices  42.2 us (25%)
  Pallas kernels  10.2 us (6%)
  local copies, waits for them, and re-layouts  6.75 us (4%)
    all_to_all x3, waiting for transfers between devices, exchange(): return lax.all_to_all(pieces, axis, 0, 0, tiled=True)  37.2 us
    all_gather x1, blocking collectives, on_device(): gathered = lax.all_gather(scaled_sum(received, gain.T), 'b', axis=0)  26.9 us
    ppermute x4, starting transfers between devices, to_row(): return lax.ppermute(piece, ('section', 'b'), route)  23.6 us
    all_to_all x1, blocking collectives, exchange(): return lax.all_to_all(pieces, axis, 0, 0, tiled=True)  17.6 us
    ppermute x4, waiting for transfers between devices, to_row(): return lax.ppermute(piece, ('section', 'b'), route)  13.9 us
    all_to_all x3, starting transfers between devices, exchange(): return lax.all_to_all(pieces, axis, 0, 0, tiled=True)  13.5 us
    ppermute x1, waiting for transfers between devices, on_device(): other = lax.ppermute(gathered, 'z', [(0, 1), (1, 0)])  13 us
    unnamed x16, local copies, waits for them, and re-layouts  6.62 us
  transfers between devices with their start and end apart: 8, of which 6 were waited for; matrix products, arithmetic and copies ran while one was open for 0% of the time, Pallas kernels for 3%

profile of v3, /device:TPU:6, one launch (start us, length us, event | category | flops | bytes accessed | tf_op | source)
XLA Modules:
  0.0 168.2 jit_solution(14168049440058562663)
XLA Ops:
  0.0 1.6 copy-done.2
  2.4 1.6 out_pieces.1
  4.1 1.5 copy-done
  5.6 5.8 %all-to-all-start = ((bf16[8,128,1280]{2,1,0:T(8,128)(2,1)}), bf16[8,128,1280]{2,1,0:T(8,128)(2,1)S(1)}, u32[]{:S(2)}, u32[]{:S(2)}) async-start(bf16[8,128,1280]{2,1,0:T(8,128)(2,1)} %copy-done), calls=%async_computation | async-start | bytes 5242880 | tf_op jit(solution)/shard_map/all_to_all | solution.py:24
  11.4 4.2 %in_pieces.1 = bf16[4,2560,128]{2,1,0:T(8,128)(2,1)} custom-call(s32[1]{0:T(128)} %bitcast.side_ref, bf16[1,8192,128]{2,1,0:T(8,128)(2,1)} %refs_7_.1, bf16[1,8192,128]{2,1,0:T(8,128)(2,1)} %refs_7_.1, bf16[1,8192,128]{2,1,0:T(8,128)(2,1)} %refs_7_.1, bf16[1,8192,128]{2,1,0:T(8,128)(2,1)} %refs_7_.1, bf16[1,8192,128]{2,1,0:T(8,128)(2,1)} %refs_7_.1, ...), custom_call_target="tpu_custom_call" | custom-call | tf_op jit(solution)/shard_map/in_pieces/pallas_call | solution.py:122
  15.7 27.4 %all-to-all-done.got_ref = bf16[8,128,1280]{2,1,0:T(8,128)(2,1)S(1)} async-done(((bf16[8,128,1280]{2,1,0:T(8,128)(2,1)}), bf16[8,128,1280]{2,1,0:T(8,128)(2,1)S(1)}, u32[]{:S(2)}, u32[]{:S(2)}) %all-to-all-start) | async-done | bytes 2621472 | tf_op jit(solution)/shard_map/all_to_all | solution.py:24
  43.1 1.3 row_terms.1
  44.4 3.8 %all-to-all-start.1 = ((bf16[4,2560,128]{2,1,0:T(8,128)(2,1)}), bf16[4,2560,128]{2,1,0:T(8,128)(2,1)S(1)}, u32[]{:S(2)}, u32[]{:S(2)}) async-start(bf16[4,2560,128]{2,1,0:T(8,128)(2,1)} %in_pieces.1), calls=%async_computation.1 | async-start | bytes 5242880 | tf_op jit(solution)/shard_map/all_to_all | solution.py:24
  48.2 1.9 %collective-permute-start = (bf16[256,256]{1,0:T(8,128)(2,1)}, bf16[256,256]{1,0:T(8,128)(2,1)S(1)}, u32[]{:S(2)}, u32[]{:S(2)}) collective-permute-start(bf16[256,256]{1,0:T(8,128)(2,1)} %get-tuple-element.21), channel_id=1, source_target_pairs={{0,32},{8,40},{16,48},{24,56},{32,64},{40,72},{48,80},{56,88},{64,... | collective-permute-start | bytes 393224 | tf_op jit(solution)/shard_map/ppermute | solution.py:264
  50.2 16.0 %collective-permute-start.1 = (bf16[256,256]{1,0:T(8,128)(2,1)}, bf16[256,256]{1,0:T(8,128)(2,1)S(1)}, u32[]{:S(2)}, u32[]{:S(2)}) collective-permute-start(bf16[256,256]{1,0:T(8,128)(2,1)} %get-tuple-element.22), channel_id=1, source_target_pairs={{0,40},{8,32},{16,56},{24,48},{32,72},{40,64},{48,88},{56,80},{64,... | collective-permute-start | bytes 393224 | tf_op jit(solution)/shard_map/ppermute | solution.py:264
  66.2 2.8 %collective-permute-start.2 = (bf16[256,256]{1,0:T(8,128)(2,1)S(1)}, bf16[256,256]{1,0:T(8,128)(2,1)S(1)}, u32[]{:S(2)}, u32[]{:S(2)}) collective-permute-start(bf16[256,256]{1,0:T(8,128)(2,1)S(1)} %get-tuple-element.23), channel_id=1, source_target_pairs={{0,48},{8,56},{16,32},{24,40},{32,80},{40,88},{48,64},{56,72},{64,... | collective-permute-start | bytes 393224 | tf_op jit(solution)/shard_map/ppermute | solution.py:264
  69.0 2.8 %collective-permute-start.3 = (bf16[256,256]{1,0:T(8,128)(2,1)S(1)}, bf16[256,256]{1,0:T(8,128)(2,1)S(1)}, u32[]{:S(2)}, u32[]{:S(2)}) collective-permute-start(bf16[256,256]{1,0:T(8,128)(2,1)S(1)} %get-tuple-element.24), channel_id=1, source_target_pairs={{0,56},{8,48},{16,40},{24,32},{32,88},{40,80},{48,72},{56,64},{64,... | collective-permute-start | bytes 393224 | tf_op jit(solution)/shard_map/ppermute | solution.py:264
  72.0 3.8 %collective-permute-done.1.refs_1_ = bf16[256,256]{1,0:T(8,128)(2,1)S(1)} collective-permute-done((bf16[256,256]{1,0:T(8,128)(2,1)}, bf16[256,256]{1,0:T(8,128)(2,1)S(1)}, u32[]{:S(2)}, u32[]{:S(2)}) %collective-permute-start.1) | collective-permute-done | bytes 131104 | tf_op jit(solution)/shard_map/ppermute | solution.py:264
  75.8 7.6 %collective-permute-done.2.refs_2_ = bf16[256,256]{1,0:T(8,128)(2,1)S(1)} collective-permute-done((bf16[256,256]{1,0:T(8,128)(2,1)S(1)}, bf16[256,256]{1,0:T(8,128)(2,1)S(1)}, u32[]{:S(2)}, u32[]{:S(2)}) %collective-permute-start.2) | collective-permute-done | bytes 131104 | tf_op jit(solution)/shard_map/ppermute | solution.py:264
  83.4 2.5 %collective-permute-done.3.refs_3_ = bf16[256,256]{1,0:T(8,128)(2,1)S(1)} collective-permute-done((bf16[256,256]{1,0:T(8,128)(2,1)S(1)}, bf16[256,256]{1,0:T(8,128)(2,1)S(1)}, u32[]{:S(2)}, u32[]{:S(2)}) %collective-permute-start.3) | collective-permute-done | bytes 131104 | tf_op jit(solution)/shard_map/ppermute | solution.py:264
  86.0 26.9 %all-gather = bf16[1088,256]{1,0:T(8,128)(2,1)S(1)} all-gather(bf16[272,256]{1,0:T(8,128)(2,1)S(1)} %scaled_sum.1), channel_id=2, replica_groups=mesh['section'=16,'b'=4,'z'=2,'y'=4] {'b'}, dimensions={0}, use_global_device_ids=true | all-gather | bytes 696320 | tf_op jit(solution)/shard_map/all_gather | solution.py:279
  112.9 5.1 %collective-permute-start.4 = (bf16[4,272,256]{2,1,0:T(8,128)(2,1)S(1)}, bf16[4,272,256]{2,1,0:T(8,128)(2,1)S(1)}, u32[]{:S(2)}, u32[]{:S(2)}) collective-permute-start(bf16[4,272,256]{2,1,0:T(8,128)(2,1)S(1)} %bitcast.7), channel_id=1, source_target_pairs={{0,4},{4,0},{1,5},{5,1},{2,6},{6,2},{3,7},{7,3},{8,12},{12,8},{9,1... | collective-permute-start | bytes 1671176 | tf_op jit(solution)/shard_map/ppermute | solution.py:280
  118.0 13.0 %collective-permute-done.4.other_ref = bf16[4,272,256]{2,1,0:T(8,128)(2,1)S(1)} collective-permute-done((bf16[4,272,256]{2,1,0:T(8,128)(2,1)S(1)}, bf16[4,272,256]{2,1,0:T(8,128)(2,1)S(1)}, u32[]{:S(2)}, u32[]{:S(2)}) %collective-permute-start.4) | collective-permute-done | bytes 557088 | tf_op jit(solution)/shard_map/ppermute | solution.py:280
  131.8 1.1 copy-done.4
  132.8 1.6 projections.1
  135.3 3.9 %all-to-all-start.2 = ((bf16[4,272,256]{2,1,0:T(8,128)(2,1)}), bf16[4,272,256]{2,1,0:T(8,128)(2,1)S(1)}, u32[]{:S(2)}, u32[]{:S(2)}) async-start(bf16[4,272,256]{2,1,0:T(8,128)(2,1)} %copy-done.1), calls=%async_computation.2 | async-start | bytes 1114112 | tf_op jit(solution)/shard_map/all_to_all | solution.py:24
  139.5 9.8 %all-to-all-done.2.got_ref = bf16[4,272,256]{2,1,0:T(8,128)(2,1)S(1)} async-done(((bf16[4,272,256]{2,1,0:T(8,128)(2,1)}), bf16[4,272,256]{2,1,0:T(8,128)(2,1)S(1)}, u32[]{:S(2)}, u32[]{:S(2)}) %all-to-all-start.2) | async-done | bytes 557088 | tf_op jit(solution)/shard_map/all_to_all | solution.py:24
  149.4 17.6 %all_to_all.20.pairs_ref = bf16[8,32,256]{2,1,0:T(8,128)(2,1)S(1)} all-to-all(bf16[8,32,256]{2,1,0:T(8,128)(2,1)S(1)} %get-tuple-element.26), channel_id=1, replica_groups=mesh['section'=16,'b'=4,'z'=2,'y'=4] {'b','z'}, dimensions={0} | all-to-all | bytes 262144 | tf_op jit(solution)/shard_map/all_to_all | solution.py:24
  167.0 1.2 attention.1
  (21 shorter events, 3.1 us)
Async XLA Ops:
  0.0 1.6 copy-start.2
  1.6 0.8 copy-start.6
  4.1 1.5 copy-start
  5.6 37.5 %all-to-all-start = ((bf16[8,128,1280]{2,1,0:T(8,128)(2,1)}), bf16[8,128,1280]{2,1,0:T(8,128)(2,1)S(1)}, u32[]{:S(2)}, u32[]{:S(2)}) async-start(bf16[8,128,1280]{2,1,0:T(8,128)(2,1)} %copy-done), calls=%async_computation | async-start | bytes 5242880 | tf_op jit(solution)/shard_map/all_to_all | solution.py:24
  11.4 31.7 %copy-start.5 = (bf16[1,256,256]{2,1,0:T(8,128)(2,1)S(1)}, bf16[1,256,256]{2,1,0:T(8,128)(2,1)}, u32[]{:S(2)}) copy-start(bf16[1,256,256]{2,1,0:T(8,128)(2,1)} %residual_ref.1) | copy-start | bytes 393220
  44.4 27.4 %copy-start.7 = (f32[1,256]{1,0:T(1,128)S(1)}, f32[1,256]{1,0:T(1,128)}, u32[]{:S(2)}) copy-start(f32[1,256]{1,0:T(1,128)} %param.9) | copy-start | bytes 3076
  44.4 87.3 %all-to-all-start.1 = ((bf16[4,2560,128]{2,1,0:T(8,128)(2,1)}), bf16[4,2560,128]{2,1,0:T(8,128)(2,1)S(1)}, u32[]{:S(2)}, u32[]{:S(2)}) async-start(bf16[4,2560,128]{2,1,0:T(8,128)(2,1)} %in_pieces.1), calls=%async_computation.1 | async-start | bytes 5242880 | tf_op jit(solution)/shard_map/all_to_all | solution.py:24
  48.2 23.8 %collective-permute-start = (bf16[256,256]{1,0:T(8,128)(2,1)}, bf16[256,256]{1,0:T(8,128)(2,1)S(1)}, u32[]{:S(2)}, u32[]{:S(2)}) collective-permute-start(bf16[256,256]{1,0:T(8,128)(2,1)} %get-tuple-element.21), channel_id=1, source_target_pairs={{0,32},{8,40},{16,48},{24,56},{32,64},{40,72},{48,80},{56,88},{64,... | collective-permute-start | bytes 393224 | tf_op jit(solution)/shard_map/ppermute | solution.py:264
  50.2 25.6 %collective-permute-start.1 = (bf16[256,256]{1,0:T(8,128)(2,1)}, bf16[256,256]{1,0:T(8,128)(2,1)S(1)}, u32[]{:S(2)}, u32[]{:S(2)}) collective-permute-start(bf16[256,256]{1,0:T(8,128)(2,1)} %get-tuple-element.22), channel_id=1, source_target_pairs={{0,40},{8,32},{16,56},{24,48},{32,72},{40,64},{48,88},{56,80},{64,... | collective-permute-start | bytes 393224 | tf_op jit(solution)/shard_map/ppermute | solution.py:264
  66.2 17.2 %collective-permute-start.2 = (bf16[256,256]{1,0:T(8,128)(2,1)S(1)}, bf16[256,256]{1,0:T(8,128)(2,1)S(1)}, u32[]{:S(2)}, u32[]{:S(2)}) collective-permute-start(bf16[256,256]{1,0:T(8,128)(2,1)S(1)} %get-tuple-element.23), channel_id=1, source_target_pairs={{0,48},{8,56},{16,32},{24,40},{32,80},{40,88},{48,64},{56,72},{64,... | collective-permute-start | bytes 393224 | tf_op jit(solution)/shard_map/ppermute | solution.py:264
  69.0 16.9 %collective-permute-start.3 = (bf16[256,256]{1,0:T(8,128)(2,1)S(1)}, bf16[256,256]{1,0:T(8,128)(2,1)S(1)}, u32[]{:S(2)}, u32[]{:S(2)}) collective-permute-start(bf16[256,256]{1,0:T(8,128)(2,1)S(1)} %get-tuple-element.24), channel_id=1, source_target_pairs={{0,56},{8,48},{16,40},{24,32},{32,88},{40,80},{48,72},{56,64},{64,... | collective-permute-start | bytes 393224 | tf_op jit(solution)/shard_map/ppermute | solution.py:264
  112.9 18.1 %collective-permute-start.4 = (bf16[4,272,256]{2,1,0:T(8,128)(2,1)S(1)}, bf16[4,272,256]{2,1,0:T(8,128)(2,1)S(1)}, u32[]{:S(2)}, u32[]{:S(2)}) collective-permute-start(bf16[4,272,256]{2,1,0:T(8,128)(2,1)S(1)} %bitcast.7), channel_id=1, source_target_pairs={{0,4},{4,0},{1,5},{5,1},{2,6},{6,2},{3,7},{7,3},{8,12},{12,8},{9,1... | collective-permute-start | bytes 1671176 | tf_op jit(solution)/shard_map/ppermute | solution.py:280
  131.0 0.8 copy-start.3
  131.8 1.1 copy-start.4
  134.5 0.8 copy-start.1
  135.3 14.0 %all-to-all-start.2 = ((bf16[4,272,256]{2,1,0:T(8,128)(2,1)}), bf16[4,272,256]{2,1,0:T(8,128)(2,1)S(1)}, u32[]{:S(2)}, u32[]{:S(2)}) async-start(bf16[4,272,256]{2,1,0:T(8,128)(2,1)} %copy-done.1), calls=%async_computation.2 | async-start | bytes 1114112 | tf_op jit(solution)/shard_map/all_to_all | solution.py:24

commit v4 on v3

--- a/solution.py
+++ b/solution.py
@@ -111,7 +111,7 @@
                 out[0, at:at + cols] = kv_refs[r][:, k * head:(k + 1) * head]
 
     def place(r, y, side_ref):
-        return r % ROWS * COLS + (side_ref[0] ^ (r // ROWS)) * LINE + y
+        return r % ROWS * COLS + (side_ref[0] ^ (r // ROWS)) * LINE + (side_ref[1] ^ y)
 
     def q_strip(r):
         return pl.BlockSpec((1, part, head), lambda y, s: (0, place(r, y, s), 0))
@@ -166,8 +166,8 @@
     return call(body, "scaled_sum", outs, [VMEM] * (ROWS + 1), *pieces, gain)
 
 
-def projections(got, own, other):
-    rows, head = got.shape[1:]
+def projections(got, own, other, line):
+    rows, head = got[0].shape
     tokens = own.shape[2]
     part = own.shape[1] - STATS
     half = ROWS * part
@@ -177,32 +177,34 @@
     each = cols // ROWS
     size = LINE * cols
 
-    def body(got_ref, own_ref, other_ref, out):
+    def body(line_ref, *refs):
+        got_refs, (own_ref, other_ref, out) = refs[:LINE], refs[LINE:]
         sides = [ref[:, :part].reshape(half, tokens) for ref in (own_ref, other_ref)]
         features = jnp.concatenate(sides, axis=0)
         kv = jnp.zeros((size, tokens), F32)
         for k in range(chunks):
             at = block + k * cols
-            weight = got_ref[:, at:at + cols].reshape(size, head)
+            weight = jnp.concatenate([ref[at:at + cols] for ref in got_refs], axis=0)
             kv = kv + contract(weight, features[k * head:(k + 1) * head], 1, 0)
         to = lax.broadcasted_iota(jnp.int32, (size, size), 0)
         source = lax.broadcasted_iota(jnp.int32, (size, size), 1)
         group, rest = to // (LINE * each), to % (LINE * each)
         kind, rest = rest // (LINE * each // 2), rest % (LINE * each // 2)
         column, feature = rest // (each // 2), rest % (each // 2)
-        wanted = column * cols + group * each + kind * (each // 2) + feature
+        wanted = (column ^ line_ref[0]) * cols + group * each + kind * (each // 2) + feature
         select = jnp.where(source == wanted, 1.0, 0.0).astype(BF16)
         kv = contract(select, kv.astype(BF16), 1, 0).astype(BF16)
         squares = own_ref[:, part:].astype(F32) + other_ref[:, part:].astype(F32)
         squares = jnp.sum(jnp.sum(squares, axis=0), axis=0, keepdims=True)
         stats = stats_rows(squares)
         for y in range(LINE):
-            out[y, :head] = contract(got_ref[y, :block], features, 0, 0).astype(BF16)
+            out[line_ref[0] ^ y, :head] = contract(got_refs[y][:block], features, 0, 0).astype(BF16)
             out[y, head:head + size] = kv
             out[y, head + size:] = stats
 
     outs = jax.ShapeDtypeStruct((LINE, head + size + STATS, tokens), BF16)
-    return call(body, "projections", outs, [VMEM] * 3, got, own, other)
+    specs = [SMEM] + [VMEM] * (LINE + 2)
+    return call(body, "projections", outs, specs, line, *got, own, other)
 
 
 def head_inputs(got, cosine, sine, width):
@@ -253,6 +255,7 @@
     tokens, head = context.shape[1:]
     width = out_weight.shape[2]
     row = lax.axis_index("b").reshape(1)
+    line = lax.axis_index("y").reshape(1)
     sections = lax.axis_size("section")
 
     def to_row(piece, step, distance):
@@ -266,9 +269,10 @@
     got = exchange(out_pieces(out_weight, context), ("z", "y"))
     terms = row_terms(got, residual, row)
 
-    pieces = in_pieces(q_weight, kv_weight[0].T, lax.axis_index("z").reshape(1))
-    pieces, *terms = lax.optimization_barrier((pieces, *terms))
-    weights = exchange(pieces, "y")
+    pieces = in_pieces(q_weight, kv_weight[0].T, jnp.stack([lax.axis_index("z"), line[0]]))
+    weights = [pieces[0]]
+    for k in range(1, LINE):
+        weights.append(lax.ppermute(pieces[k], "y", [(y, y ^ k) for y in range(LINE)]))
 
     positions = jnp.arange(tokens).astype(F32)
     frequency = THETA ** (-(jnp.arange(head // 2).astype(F32) * 2.0 / head))
@@ -278,7 +282,7 @@
     received = [to_row(terms[k], k, 1) for k in range(ROWS)]
     gathered = lax.all_gather(scaled_sum(received, gain.T), "b", axis=0)
     other = lax.ppermute(gathered, "z", [(0, 1), (1, 0)])
-    summed = exchange(projections(weights, gathered, other), "y")
+    summed = exchange(projections(weights, gathered, other, line), "y")
     queries, pairs = head_inputs(summed, cosine, sine, width)
     return attention(queries, exchange(pairs, ("b", "z")), cosine, sine)
 

time: 169 us -> 164 us (0.970); the launches traced: 168 us -> 161 us
  waiting for transfers between devices: 64.1 us -> 49.1 us
  starting transfers between devices: 42.2 us -> 53.6 us
  blocking collectives: 44.5 us -> 40.8 us
    ppermute x4, waiting for transfers between devices: 13.9 us -> 1.91 us  [to_row(): return lax.ppermute(piece, ('section', 'b'), route)]
    ppermute x0 -> x3, starting transfers between devices: none -> 10.4 us  [on_device(): lax.ppermute(pieces[k], 'y', [(y, y ^ k) for y in range(LINE)])]
    all_gather x1, blocking collectives: 26.9 us -> 23.7 us  [on_device(): gathered = lax.all_gather(scaled_sum(received, gain.T), 'b', axis=0)]
    ppermute x1, starting transfers between devices: 5.11 us -> 7.93 us  [on_device(): other = lax.ppermute(gathered, 'z', [(0, 1), (1, 0)])]
    unnamed x16 -> x12, local copies, waits for them, and re-layouts: 6.62 us -> 3.93 us
    all_to_all x3 -> x2, starting transfers between devices: 13.5 us -> 11.5 us  [exchange(): return lax.all_to_all(pieces, axis, 0, 0, tiled=True)]
    all_to_all x3 -> x2, waiting for transfers between devices: 37.2 us -> 35.6 us  [exchange(): return lax.all_to_all(pieces, axis, 0, 0, tiled=True)]
  transfers between devices with their start and end apart: 8 -> 10, of which waited for: 6 -> 4; matrix products, arithmetic and copies ran while one was open for 0% -> 1% of each run, Pallas kernels for 3% -> 3%
where the time goes in v4:
time: 164 us; the launch traced here: 161 us
  starting transfers between devices  53.6 us (33%)
  waiting for transfers between devices  49.1 us (30%)
  blocking collectives  40.8 us (25%)
  Pallas kernels  11.3 us (7%)
  local copies, waits for them, and re-layouts  5.32 us (3%)
    all_to_all x2, waiting for transfers between devices, exchange(): return lax.all_to_all(pieces, axis, 0, 0, tiled=True)  35.6 us
    ppermute x4, starting transfers between devices, to_row(): return lax.ppermute(piece, ('section', 'b'), route)  23.7 us
    all_gather x1, blocking collectives, on_device(): gathered = lax.all_gather(scaled_sum(received, gain.T), 'b', axis=0)  23.7 us
    all_to_all x1, blocking collectives, exchange(): return lax.all_to_all(pieces, axis, 0, 0, tiled=True)  17.1 us
    ppermute x1, waiting for transfers between devices, on_device(): other = lax.ppermute(gathered, 'z', [(0, 1), (1, 0)])  11.6 us
    all_to_all x2, starting transfers between devices, exchange(): return lax.all_to_all(pieces, axis, 0, 0, tiled=True)  11.5 us
    ppermute x3, starting transfers between devices, on_device(): lax.ppermute(pieces[k], 'y', [(y, y ^ k) for y in range(LINE)])  10.4 us
    ppermute x1, starting transfers between devices, on_device(): other = lax.ppermute(gathered, 'z', [(0, 1), (1, 0)])  7.93 us
  transfers between devices with their start and end apart: 10, of which 4 were waited for; matrix products, arithmetic and copies ran while one was open for 1% of the time, Pallas kernels for 3%

profile of v4, /device:TPU:6, one launch (start us, length us, event | category | flops | bytes accessed | tf_op | source)
XLA Modules:
  0.0 161.2 jit_solution(6613459587971792054)
XLA Ops:
  0.0 1.6 copy-done.1
  1.6 0.8 copy-done.3
  2.4 1.6 %out_pieces.1 = bf16[8,128,1280]{2,1,0:T(8,128)(2,1)S(1)} custom-call(bf16[1,128,8192]{2,1,0:T(8,128)(2,1)S(1)} %copy-done.1, bf16[1,256,128]{2,1,0:T(8,128)(2,1)S(1)} %copy-done.3), custom_call_target="tpu_custom_call" | custom-call | tf_op jit(solution)/shard_map/out_pieces/pallas_call | solution.py:82
  4.1 1.5 copy-done
  5.6 5.8 %all-to-all-start = ((bf16[8,128,1280]{2,1,0:T(8,128)(2,1)}), bf16[8,128,1280]{2,1,0:T(8,128)(2,1)S(1)}, u32[]{:S(2)}, u32[]{:S(2)}) async-start(bf16[8,128,1280]{2,1,0:T(8,128)(2,1)} %copy-done), calls=%async_computation | async-start | bytes 5242880 | tf_op jit(solution)/shard_map/all_to_all | solution.py:24
  12.0 5.0 %in_pieces.1 = bf16[4,2560,128]{2,1,0:T(8,128)(2,1)} custom-call(s32[2]{0:T(128)} %pad_add_fusion.side_ref, bf16[1,8192,128]{2,1,0:T(8,128)(2,1)} %refs_7_.1, bf16[1,8192,128]{2,1,0:T(8,128)(2,1)} %refs_7_.1, bf16[1,8192,128]{2,1,0:T(8,128)(2,1)} %refs_7_.1, bf16[1,8192,128]{2,1,0:T(8,128)(2,1)} %refs_7_.1, bf16[1,8192,128]{2,1,0:T(8,128)(2,1)} %refs_7_.1, ...), custom_call_target="tpu_custom_call" | custom-call | tf_op jit(solution)/shard_map/in_pieces/pallas_call | solution.py:122
  17.0 26.1 %all-to-all-done.got_ref = bf16[8,128,1280]{2,1,0:T(8,128)(2,1)S(1)} async-done(((bf16[8,128,1280]{2,1,0:T(8,128)(2,1)}), bf16[8,128,1280]{2,1,0:T(8,128)(2,1)S(1)}, u32[]{:S(2)}, u32[]{:S(2)}) %all-to-all-start) | async-done | bytes 2621472 | tf_op jit(solution)/shard_map/all_to_all | solution.py:24
  43.8 2.1 %collective-permute-start.3 = (bf16[256,256]{1,0:T(8,128)(2,1)S(1)}, bf16[256,256]{1,0:T(8,128)(2,1)S(1)}, u32[]{:S(2)}, u32[]{:S(2)}) collective-permute-start(bf16[256,256]{1,0:T(8,128)(2,1)S(1)} %get-tuple-element.11), channel_id=1, source_target_pairs={{0,32},{8,40},{16,48},{24,56},{32,64},{40,72},{48,80},{56,88},{64,... | collective-permute-start | bytes 393224 | tf_op jit(solution)/shard_map/ppermute | solution.py:267
  45.9 16.0 %collective-permute-start.4 = (bf16[256,256]{1,0:T(8,128)(2,1)S(1)}, bf16[256,256]{1,0:T(8,128)(2,1)S(1)}, u32[]{:S(2)}, u32[]{:S(2)}) collective-permute-start(bf16[256,256]{1,0:T(8,128)(2,1)S(1)} %get-tuple-element.12), channel_id=1, source_target_pairs={{0,40},{8,32},{16,56},{24,48},{32,72},{40,64},{48,88},{56,80},{64,... | collective-permute-start | bytes 393224 | tf_op jit(solution)/shard_map/ppermute | solution.py:267
  61.9 2.8 %collective-permute-start.5 = (bf16[256,256]{1,0:T(8,128)(2,1)S(1)}, bf16[256,256]{1,0:T(8,128)(2,1)S(1)}, u32[]{:S(2)}, u32[]{:S(2)}) collective-permute-start(bf16[256,256]{1,0:T(8,128)(2,1)S(1)} %get-tuple-element.13), channel_id=1, source_target_pairs={{0,48},{8,56},{16,32},{24,40},{32,80},{40,88},{48,64},{56,72},{64,... | collective-permute-start | bytes 393224 | tf_op jit(solution)/shard_map/ppermute | solution.py:267
  64.8 2.8 %collective-permute-start.6 = (bf16[256,256]{1,0:T(8,128)(2,1)S(1)}, bf16[256,256]{1,0:T(8,128)(2,1)S(1)}, u32[]{:S(2)}, u32[]{:S(2)}) collective-permute-start(bf16[256,256]{1,0:T(8,128)(2,1)S(1)} %get-tuple-element.14), channel_id=1, source_target_pairs={{0,56},{8,48},{16,40},{24,32},{32,88},{40,80},{48,72},{56,64},{64,... | collective-permute-start | bytes 393224 | tf_op jit(solution)/shard_map/ppermute | solution.py:267
  67.6 1.2 slice_bitcast_fusion
  68.8 2.8 %collective-permute-start = (bf16[2560,128]{1,0:T(8,128)(2,1)}, bf16[2560,128]{1,0:T(8,128)(2,1)S(1)}, u32[]{:S(2)}, u32[]{:S(2)}) collective-permute-start(bf16[2560,128]{1,0:T(8,128)(2,1)} %get-tuple-element.19), channel_id=1, source_target_pairs={{0,1},{1,0},{2,3},{3,2},{4,5},{5,4},{6,7},{7,6},{8,9},{9,8},{10,11... | collective-permute-start | bytes 1966088 | tf_op jit(solution)/shard_map/ppermute | solution.py:275
  71.8 4.4 %collective-permute-start.1 = (bf16[2560,128]{1,0:T(8,128)(2,1)}, bf16[2560,128]{1,0:T(8,128)(2,1)S(1)}, u32[]{:S(2)}, u32[]{:S(2)}) collective-permute-start(bf16[2560,128]{1,0:T(8,128)(2,1)} %get-tuple-element.18), channel_id=1, source_target_pairs={{0,2},{1,3},{2,0},{3,1},{4,6},{5,7},{6,4},{7,5},{8,10},{9,11},{10,... | collective-permute-start | bytes 1966088 | tf_op jit(solution)/shard_map/ppermute | solution.py:275
  76.2 3.2 %collective-permute-start.2 = (bf16[2560,128]{1,0:T(8,128)(2,1)S(1)}, bf16[2560,128]{1,0:T(8,128)(2,1)S(1)}, u32[]{:S(2)}, u32[]{:S(2)}) collective-permute-start(bf16[2560,128]{1,0:T(8,128)(2,1)S(1)} %get-tuple-element.17), channel_id=1, source_target_pairs={{0,3},{1,2},{2,1},{3,0},{4,7},{5,6},{6,5},{7,4},{8,11},{9,10},{10,... | collective-permute-start | bytes 1966088 | tf_op jit(solution)/shard_map/ppermute | solution.py:275
  79.5 1.9 %collective-permute-done.6.refs_3_ = bf16[256,256]{1,0:T(8,128)(2,1)S(1)} collective-permute-done((bf16[256,256]{1,0:T(8,128)(2,1)S(1)}, bf16[256,256]{1,0:T(8,128)(2,1)S(1)}, u32[]{:S(2)}, u32[]{:S(2)}) %collective-permute-start.6) | collective-permute-done | bytes 131104 | tf_op jit(solution)/shard_map/ppermute | solution.py:267
  81.5 23.7 %all-gather = bf16[1088,256]{1,0:T(8,128)(2,1)S(1)} all-gather(bf16[272,256]{1,0:T(8,128)(2,1)S(1)} %scaled_sum.1), channel_id=2, replica_groups=mesh['section'=16,'b'=4,'z'=2,'y'=4] {'b'}, dimensions={0}, use_global_device_ids=true | all-gather | bytes 696320 | tf_op jit(solution)/shard_map/all_gather | solution.py:283
  105.2 7.9 %collective-permute-start.7 = (bf16[4,272,256]{2,1,0:T(8,128)(2,1)S(1)}, bf16[4,272,256]{2,1,0:T(8,128)(2,1)S(1)}, u32[]{:S(2)}, u32[]{:S(2)}) collective-permute-start(bf16[4,272,256]{2,1,0:T(8,128)(2,1)S(1)} %bitcast.16), channel_id=1, source_target_pairs={{0,4},{4,0},{1,5},{5,1},{2,6},{6,2},{3,7},{7,3},{8,12},{12,8},{9,1... | collective-permute-start | bytes 1671176 | tf_op jit(solution)/shard_map/ppermute | solution.py:284
  113.1 11.6 %collective-permute-done.7.refs_5_ = bf16[4,272,256]{2,1,0:T(8,128)(2,1)S(1)} collective-permute-done((bf16[4,272,256]{2,1,0:T(8,128)(2,1)S(1)}, bf16[4,272,256]{2,1,0:T(8,128)(2,1)S(1)}, u32[]{:S(2)}, u32[]{:S(2)}) %collective-permute-start.7) | collective-permute-done | bytes 557088 | tf_op jit(solution)/shard_map/ppermute | solution.py:284
  124.7 2.5 %projections.1 = bf16[4,272,256]{2,1,0:T(8,128)(2,1)} custom-call(s32[1]{0:T(128)} %bitcast.line_ref, bf16[2560,128]{1,0:T(8,128)(2,1)S(1)} %get-tuple-element.20.refs_0_, bf16[2560,128]{1,0:T(8,128)(2,1)S(1)} %collective-permute-done.refs_1_, bf16[2560,128]{1,0:T(8,128)(2,1)S(1)} %collective-permute-done.1.refs_2_, ...), custom_call_target="tpu_custom_call" | custom-call | tf_op jit(solution)/shard_map/projections/pallas_call | solution.py:43
  127.3 5.7 %all-to-all-start.1 = ((bf16[4,272,256]{2,1,0:T(8,128)(2,1)}), bf16[4,272,256]{2,1,0:T(8,128)(2,1)S(1)}, u32[]{:S(2)}, u32[]{:S(2)}) async-start(bf16[4,272,256]{2,1,0:T(8,128)(2,1)} %projections.1), calls=%async_computation.1 | async-start | bytes 1114112 | tf_op jit(solution)/shard_map/all_to_all | solution.py:24
  133.3 9.5 %all-to-all-done.1.got_ref = bf16[4,272,256]{2,1,0:T(8,128)(2,1)S(1)} async-done(((bf16[4,272,256]{2,1,0:T(8,128)(2,1)}), bf16[4,272,256]{2,1,0:T(8,128)(2,1)S(1)}, u32[]{:S(2)}, u32[]{:S(2)}) %all-to-all-start.1) | async-done | bytes 557088 | tf_op jit(solution)/shard_map/all_to_all | solution.py:24
  142.9 17.1 %all_to_all.15.pairs_ref = bf16[8,32,256]{2,1,0:T(8,128)(2,1)S(1)} all-to-all(bf16[8,32,256]{2,1,0:T(8,128)(2,1)S(1)} %get-tuple-element.16), channel_id=1, replica_groups=mesh['section'=16,'b'=4,'z'=2,'y'=4] {'b','z'}, dimensions={0} | all-to-all | bytes 262144 | tf_op jit(solution)/shard_map/all_to_all | solution.py:24
  160.0 1.2 attention.1
  (23 shorter events, 2.0 us)
Async XLA Ops:
  0.0 1.6 copy-start.1
  1.6 0.8 copy-start.3
  4.1 1.5 copy-start
  5.6 37.5 %all-to-all-start = ((bf16[8,128,1280]{2,1,0:T(8,128)(2,1)}), bf16[8,128,1280]{2,1,0:T(8,128)(2,1)S(1)}, u32[]{:S(2)}, u32[]{:S(2)}) async-start(bf16[8,128,1280]{2,1,0:T(8,128)(2,1)} %copy-done), calls=%async_computation | async-start | bytes 5242880 | tf_op jit(solution)/shard_map/all_to_all | solution.py:24
  12.0 31.1 %copy-start.2 = (bf16[1,256,256]{2,1,0:T(8,128)(2,1)S(1)}, bf16[1,256,256]{2,1,0:T(8,128)(2,1)}, u32[]{:S(2)}) copy-start(bf16[1,256,256]{2,1,0:T(8,128)(2,1)} %residual_ref.1) | copy-start | bytes 393220
  43.1 24.5 %copy-start.4 = (bf16[4,2560,128]{2,1,0:T(8,128)(2,1)S(1)}, bf16[4,2560,128]{2,1,0:T(8,128)(2,1)}, u32[]{:S(2)}) copy-start(bf16[4,2560,128]{2,1,0:T(8,128)(2,1)} %in_pieces.1) | copy-start | bytes 7864324
  43.8 27.9 %collective-permute-start.3 = (bf16[256,256]{1,0:T(8,128)(2,1)S(1)}, bf16[256,256]{1,0:T(8,128)(2,1)S(1)}, u32[]{:S(2)}, u32[]{:S(2)}) collective-permute-start(bf16[256,256]{1,0:T(8,128)(2,1)S(1)} %get-tuple-element.11), channel_id=1, source_target_pairs={{0,32},{8,40},{16,48},{24,56},{32,64},{40,72},{48,80},{56,88},{64,... | collective-permute-start | bytes 393224 | tf_op jit(solution)/shard_map/ppermute | solution.py:267
  45.9 30.3 %collective-permute-start.4 = (bf16[256,256]{1,0:T(8,128)(2,1)S(1)}, bf16[256,256]{1,0:T(8,128)(2,1)S(1)}, u32[]{:S(2)}, u32[]{:S(2)}) collective-permute-start(bf16[256,256]{1,0:T(8,128)(2,1)S(1)} %get-tuple-element.12), channel_id=1, source_target_pairs={{0,40},{8,32},{16,56},{24,48},{32,72},{40,64},{48,88},{56,80},{64,... | collective-permute-start | bytes 393224 | tf_op jit(solution)/shard_map/ppermute | solution.py:267
  61.9 17.6 %collective-permute-start.5 = (bf16[256,256]{1,0:T(8,128)(2,1)S(1)}, bf16[256,256]{1,0:T(8,128)(2,1)S(1)}, u32[]{:S(2)}, u32[]{:S(2)}) collective-permute-start(bf16[256,256]{1,0:T(8,128)(2,1)S(1)} %get-tuple-element.13), channel_id=1, source_target_pairs={{0,48},{8,56},{16,32},{24,40},{32,80},{40,88},{48,64},{56,72},{64,... | collective-permute-start | bytes 393224 | tf_op jit(solution)/shard_map/ppermute | solution.py:267
  64.7 6.9 %copy-start.5 = (f32[1,256]{1,0:T(1,128)S(1)}, f32[1,256]{1,0:T(1,128)}, u32[]{:S(2)}) copy-start(f32[1,256]{1,0:T(1,128)} %param.9) | copy-start | bytes 3076
  64.8 16.6 %collective-permute-start.6 = (bf16[256,256]{1,0:T(8,128)(2,1)S(1)}, bf16[256,256]{1,0:T(8,128)(2,1)S(1)}, u32[]{:S(2)}, u32[]{:S(2)}) collective-permute-start(bf16[256,256]{1,0:T(8,128)(2,1)S(1)} %get-tuple-element.14), channel_id=1, source_target_pairs={{0,56},{8,48},{16,40},{24,32},{32,88},{40,80},{48,72},{56,64},{64,... | collective-permute-start | bytes 393224 | tf_op jit(solution)/shard_map/ppermute | solution.py:267
  68.8 44.3 %collective-permute-start = (bf16[2560,128]{1,0:T(8,128)(2,1)}, bf16[2560,128]{1,0:T(8,128)(2,1)S(1)}, u32[]{:S(2)}, u32[]{:S(2)}) collective-permute-start(bf16[2560,128]{1,0:T(8,128)(2,1)} %get-tuple-element.19), channel_id=1, source_target_pairs={{0,1},{1,0},{2,3},{3,2},{4,5},{5,4},{6,7},{7,6},{8,9},{9,8},{10,11... | collective-permute-start | bytes 1966088 | tf_op jit(solution)/shard_map/ppermute | solution.py:275
  71.8 41.4 %collective-permute-start.1 = (bf16[2560,128]{1,0:T(8,128)(2,1)}, bf16[2560,128]{1,0:T(8,128)(2,1)S(1)}, u32[]{:S(2)}, u32[]{:S(2)}) collective-permute-start(bf16[2560,128]{1,0:T(8,128)(2,1)} %get-tuple-element.18), channel_id=1, source_target_pairs={{0,2},{1,3},{2,0},{3,1},{4,6},{5,7},{6,4},{7,5},{8,10},{9,11},{10,... | collective-permute-start | bytes 1966088 | tf_op jit(solution)/shard_map/ppermute | solution.py:275
  76.2 36.9 %collective-permute-start.2 = (bf16[2560,128]{1,0:T(8,128)(2,1)S(1)}, bf16[2560,128]{1,0:T(8,128)(2,1)S(1)}, u32[]{:S(2)}, u32[]{:S(2)}) collective-permute-start(bf16[2560,128]{1,0:T(8,128)(2,1)S(1)} %get-tuple-element.17), channel_id=1, source_target_pairs={{0,3},{1,2},{2,1},{3,0},{4,7},{5,6},{6,5},{7,4},{8,11},{9,10},{10,... | collective-permute-start | bytes 1966088 | tf_op jit(solution)/shard_map/ppermute | solution.py:275
  105.2 19.6 %collective-permute-start.7 = (bf16[4,272,256]{2,1,0:T(8,128)(2,1)S(1)}, bf16[4,272,256]{2,1,0:T(8,128)(2,1)S(1)}, u32[]{:S(2)}, u32[]{:S(2)}) collective-permute-start(bf16[4,272,256]{2,1,0:T(8,128)(2,1)S(1)} %bitcast.16), channel_id=1, source_target_pairs={{0,4},{4,0},{1,5},{5,1},{2,6},{6,2},{3,7},{7,3},{8,12},{12,8},{9,1... | collective-permute-start | bytes 1671176 | tf_op jit(solution)/shard_map/ppermute | solution.py:284
  127.3 15.5 %all-to-all-start.1 = ((bf16[4,272,256]{2,1,0:T(8,128)(2,1)}), bf16[4,272,256]{2,1,0:T(8,128)(2,1)S(1)}, u32[]{:S(2)}, u32[]{:S(2)}) async-start(bf16[4,272,256]{2,1,0:T(8,128)(2,1)} %projections.1), calls=%async_computation.1 | async-start | bytes 1114112 | tf_op jit(solution)/shard_map/all_to_all | solution.py:24

commit v5 on v4

--- a/solution.py
+++ b/solution.py
@@ -56,39 +56,18 @@
     part = width // (ROWS * COLS)
     block = ROWS * part
 
-    def body(weight, own, out, staged, sems, out_sems):
-        def strip(a, r):
-            return pltpu.make_async_copy(
-                weight.at[0, :, pl.ds((r * COLS + a) * part, part)],
-                staged.at[a, :, pl.ds(r * part, part)],
-                sems.at[a, r],
-            )
-
-        for a in range(COLS):
-            for r in range(ROWS):
-                strip(a, r).start()
-        turned = own[0].astype(F32).T.astype(BF16)
-        for a in range(COLS):
-            staged[a, :, block:] = turned
-        outs = [pltpu.make_async_copy(staged.at[a], out.at[a], out_sems.at[a]) for a in range(COLS)]
-        for a in range(COLS):
-            for r in range(ROWS):
-                strip(a, r).wait()
-            outs[a].start()
-        for copy in outs:
-            copy.wait()
-
-    shape = (COLS, head, block + tokens)
+    def body(weight, own, out):
+        for r in range(ROWS):
+            at = pl.multiple_of((r * COLS + pl.program_id(0)) * part, part)
+            out[0, :, r * part:(r + 1) * part] = weight[0, :, pl.ds(at, part)]
+        out[0, :, block:] = own[0].astype(F32).T.astype(BF16)
+
     return pl.pallas_call(
         body,
-        in_specs=[pl.BlockSpec(memory_space=pl.ANY), VMEM],
-        out_specs=pl.BlockSpec(memory_space=pl.ANY),
-        out_shape=jax.ShapeDtypeStruct(shape, BF16),
-        scratch_shapes=[
-            pltpu.VMEM(shape, BF16),
-            pltpu.SemaphoreType.DMA((COLS, ROWS)),
-            pltpu.SemaphoreType.DMA((COLS,)),
-        ],
+        grid=(COLS,),
+        in_specs=[VMEM, VMEM],
+        out_specs=pl.BlockSpec((1, head, block + tokens), lambda a: (a, 0, 0)),
+        out_shape=jax.ShapeDtypeStruct((COLS, head, block + tokens), BF16),
         compiler_params=pltpu.CompilerParams(vmem_limit_bytes=40 * 2**20),
         name="out_pieces",
     )(out_weight, context)
@@ -279,7 +258,7 @@
     angles = frequency[:, None] * positions[None, :]
     cosine, sine = jnp.cos(angles), jnp.sin(angles)
 
-    received = [to_row(terms[k], k, 1) for k in range(ROWS)]
+    received = [to_row(terms[k], k, 1) for k in (2, 3, 1, 0)]
     gathered = lax.all_gather(scaled_sum(received, gain.T), "b", axis=0)
     other = lax.ppermute(gathered, "z", [(0, 1), (1, 0)])
     summed = exchange(projections(weights, gathered, other, line), "y")

time: 164 us -> 160 us (0.976)
  starting transfers between devices: 53.6 us -> 45.6 us
  waiting for transfers between devices: 49.1 us -> 52 us
    ppermute x4, waiting for transfers between devices: 1.91 us -> 8.51 us  [to_row(): return lax.ppermute(piece, ('section', 'b'), route)]
    ppermute x1, starting transfers between devices: 7.93 us -> 1.91 us  [on_device(): other = lax.ppermute(gathered, 'z', [(0, 1), (1, 0)])]
    ppermute x1, waiting for transfers between devices: 11.6 us -> 9.47 us  [on_device(): other = lax.ppermute(gathered, 'z', [(0, 1), (1, 0)])]
where the time goes in v5:
time: 160 us; the launch traced here: 157 us
  waiting for transfers between devices  52 us (32%)
  starting transfers between devices  45.6 us (28%)
  blocking collectives  42 us (26%)
  Pallas kernels  10.5 us (7%)
  local copies, waits for them, and re-layouts  5.32 us (3%)
    all_to_all x2, waiting for transfers between devices, exchange(): return lax.all_to_all(pieces, axis, 0, 0, tiled=True)  34 us
    all_gather x1, blocking collectives, on_device(): gathered = lax.all_gather(scaled_sum(received, gain.T), 'b', axis=0)  25 us
    ppermute x4, starting transfers between devices, to_row(): return lax.ppermute(piece, ('section', 'b'), route)  22.6 us
    all_to_all x1, blocking collectives, exchange(): return lax.all_to_all(pieces, axis, 0, 0, tiled=True)  16.9 us
    all_to_all x2, starting transfers between devices, exchange(): return lax.all_to_all(pieces, axis, 0, 0, tiled=True)  10.7 us
    ppermute x3, starting transfers between devices, on_device(): lax.ppermute(pieces[k], 'y', [(y, y ^ k) for y in range(LINE)])  10.4 us
    ppermute x1, waiting for transfers between devices, on_device(): other = lax.ppermute(gathered, 'z', [(0, 1), (1, 0)])  9.47 us
    ppermute x4, waiting for transfers between devices, to_row(): return lax.ppermute(piece, ('section', 'b'), route)  8.51 us
  transfers between devices with their start and end apart: 10, of which 4 were waited for; matrix products, arithmetic and copies ran while one was open for 1% of the time, Pallas kernels for 3%

profile of v5, /device:TPU:6, one launch (start us, length us, event | category | flops | bytes accessed | tf_op | source)
XLA Modules:
  0.0 156.5 jit_solution(2719658122651565237)
XLA Ops:
  0.0 1.6 %copy-done.1 = bf16[1,128,8192]{2,1,0:T(8,128)(2,1)S(1)} copy-done((bf16[1,128,8192]{2,1,0:T(8,128)(2,1)S(1)}, bf16[1,128,8192]{2,1,0:T(8,128)(2,1)}, u32[]{:S(2)}) %copy-start.1) | copy-done | bytes 2097176
  1.6 0.8 copy-done.3
  2.4 0.9 out_pieces.1
  3.3 1.5 copy-done
  4.8 5.8 %all-to-all-start = ((bf16[8,128,1280]{2,1,0:T(8,128)(2,1)}), bf16[8,128,1280]{2,1,0:T(8,128)(2,1)S(1)}, u32[]{:S(2)}, u32[]{:S(2)}) async-start(bf16[8,128,1280]{2,1,0:T(8,128)(2,1)} %copy-done), calls=%async_computation | async-start | bytes 5242880 | tf_op jit(solution)/shard_map/all_to_all | solution.py:24
  11.2 5.0 %in_pieces.1 = bf16[4,2560,128]{2,1,0:T(8,128)(2,1)} custom-call(s32[2]{0:T(128)} %pad_add_fusion.side_ref, bf16[1,8192,128]{2,1,0:T(8,128)(2,1)} %refs_7_.1, bf16[1,8192,128]{2,1,0:T(8,128)(2,1)} %refs_7_.1, bf16[1,8192,128]{2,1,0:T(8,128)(2,1)} %refs_7_.1, bf16[1,8192,128]{2,1,0:T(8,128)(2,1)} %refs_7_.1, bf16[1,8192,128]{2,1,0:T(8,128)(2,1)} %refs_7_.1, ...), custom_call_target="tpu_custom_call" | custom-call | tf_op jit(solution)/shard_map/in_pieces/pallas_call | solution.py:101
  16.2 26.1 %all-to-all-done.got_ref = bf16[8,128,1280]{2,1,0:T(8,128)(2,1)S(1)} async-done(((bf16[8,128,1280]{2,1,0:T(8,128)(2,1)}), bf16[8,128,1280]{2,1,0:T(8,128)(2,1)S(1)}, u32[]{:S(2)}, u32[]{:S(2)}) %all-to-all-start) | async-done | bytes 2621472 | tf_op jit(solution)/shard_map/all_to_all | solution.py:24
  43.1 8.5 %collective-permute-start.3 = (bf16[256,256]{1,0:T(8,128)(2,1)S(1)}, bf16[256,256]{1,0:T(8,128)(2,1)S(1)}, u32[]{:S(2)}, u32[]{:S(2)}) collective-permute-start(bf16[256,256]{1,0:T(8,128)(2,1)S(1)} %get-tuple-element.11), channel_id=1, source_target_pairs={{0,48},{8,56},{16,32},{24,40},{32,80},{40,88},{48,64},{56,72},{64,... | collective-permute-start | bytes 393224 | tf_op jit(solution)/shard_map/ppermute | solution.py:246
  51.6 9.6 %collective-permute-start.4 = (bf16[256,256]{1,0:T(8,128)(2,1)S(1)}, bf16[256,256]{1,0:T(8,128)(2,1)S(1)}, u32[]{:S(2)}, u32[]{:S(2)}) collective-permute-start(bf16[256,256]{1,0:T(8,128)(2,1)S(1)} %get-tuple-element.12), channel_id=1, source_target_pairs={{0,56},{8,48},{16,40},{24,32},{32,88},{40,80},{48,72},{56,64},{64,... | collective-permute-start | bytes 393224 | tf_op jit(solution)/shard_map/ppermute | solution.py:246
  61.1 2.6 %collective-permute-start.5 = (bf16[256,256]{1,0:T(8,128)(2,1)S(1)}, bf16[256,256]{1,0:T(8,128)(2,1)S(1)}, u32[]{:S(2)}, u32[]{:S(2)}) collective-permute-start(bf16[256,256]{1,0:T(8,128)(2,1)S(1)} %get-tuple-element.13), channel_id=1, source_target_pairs={{0,40},{8,32},{16,56},{24,48},{32,72},{40,64},{48,88},{56,80},{64,... | collective-permute-start | bytes 393224 | tf_op jit(solution)/shard_map/ppermute | solution.py:246
  63.8 1.9 %collective-permute-start.6 = (bf16[256,256]{1,0:T(8,128)(2,1)S(1)}, bf16[256,256]{1,0:T(8,128)(2,1)S(1)}, u32[]{:S(2)}, u32[]{:S(2)}) collective-permute-start(bf16[256,256]{1,0:T(8,128)(2,1)S(1)} %get-tuple-element.14), channel_id=1, source_target_pairs={{0,32},{8,40},{16,48},{24,56},{32,64},{40,72},{48,80},{56,88},{64,... | collective-permute-start | bytes 393224 | tf_op jit(solution)/shard_map/ppermute | solution.py:246
  65.7 1.2 slice_bitcast_fusion
  67.0 2.0 %collective-permute-start = (bf16[2560,128]{1,0:T(8,128)(2,1)}, bf16[2560,128]{1,0:T(8,128)(2,1)S(1)}, u32[]{:S(2)}, u32[]{:S(2)}) collective-permute-start(bf16[2560,128]{1,0:T(8,128)(2,1)} %get-tuple-element.19), channel_id=1, source_target_pairs={{0,1},{1,0},{2,3},{3,2},{4,5},{5,4},{6,7},{7,6},{8,9},{9,8},{10,11... | collective-permute-start | bytes 1966088 | tf_op jit(solution)/shard_map/ppermute | solution.py:254
  69.2 4.3 %collective-permute-start.1 = (bf16[2560,128]{1,0:T(8,128)(2,1)}, bf16[2560,128]{1,0:T(8,128)(2,1)S(1)}, u32[]{:S(2)}, u32[]{:S(2)}) collective-permute-start(bf16[2560,128]{1,0:T(8,128)(2,1)} %get-tuple-element.18), channel_id=1, source_target_pairs={{0,2},{1,3},{2,0},{3,1},{4,6},{5,7},{6,4},{7,5},{8,10},{9,11},{10,... | collective-permute-start | bytes 1966088 | tf_op jit(solution)/shard_map/ppermute | solution.py:254
  73.5 4.1 %collective-permute-start.2 = (bf16[2560,128]{1,0:T(8,128)(2,1)S(1)}, bf16[2560,128]{1,0:T(8,128)(2,1)S(1)}, u32[]{:S(2)}, u32[]{:S(2)}) collective-permute-start(bf16[2560,128]{1,0:T(8,128)(2,1)S(1)} %get-tuple-element.17), channel_id=1, source_target_pairs={{0,3},{1,2},{2,1},{3,0},{4,7},{5,6},{6,5},{7,4},{8,11},{9,10},{10,... | collective-permute-start | bytes 1966088 | tf_op jit(solution)/shard_map/ppermute | solution.py:254
  77.6 8.5 %collective-permute-done.6.refs_3_ = bf16[256,256]{1,0:T(8,128)(2,1)S(1)} collective-permute-done((bf16[256,256]{1,0:T(8,128)(2,1)S(1)}, bf16[256,256]{1,0:T(8,128)(2,1)S(1)}, u32[]{:S(2)}, u32[]{:S(2)}) %collective-permute-start.6) | collective-permute-done | bytes 131104 | tf_op jit(solution)/shard_map/ppermute | solution.py:246
  86.2 25.0 %all-gather = bf16[1088,256]{1,0:T(8,128)(2,1)S(1)} all-gather(bf16[272,256]{1,0:T(8,128)(2,1)S(1)} %scaled_sum.1), channel_id=2, replica_groups=mesh['section'=16,'b'=4,'z'=2,'y'=4] {'b'}, dimensions={0}, use_global_device_ids=true | all-gather | bytes 696320 | tf_op jit(solution)/shard_map/all_gather | solution.py:262
  111.2 1.9 %collective-permute-start.7 = (bf16[4,272,256]{2,1,0:T(8,128)(2,1)S(1)}, bf16[4,272,256]{2,1,0:T(8,128)(2,1)S(1)}, u32[]{:S(2)}, u32[]{:S(2)}) collective-permute-start(bf16[4,272,256]{2,1,0:T(8,128)(2,1)S(1)} %bitcast.16), channel_id=1, source_target_pairs={{0,4},{4,0},{1,5},{5,1},{2,6},{6,2},{3,7},{7,3},{8,12},{12,8},{9,1... | collective-permute-start | bytes 1671176 | tf_op jit(solution)/shard_map/ppermute | solution.py:263
  113.2 9.5 %collective-permute-done.7.refs_5_ = bf16[4,272,256]{2,1,0:T(8,128)(2,1)S(1)} collective-permute-done((bf16[4,272,256]{2,1,0:T(8,128)(2,1)S(1)}, bf16[4,272,256]{2,1,0:T(8,128)(2,1)S(1)}, u32[]{:S(2)}, u32[]{:S(2)}) %collective-permute-start.7) | collective-permute-done | bytes 557088 | tf_op jit(solution)/shard_map/ppermute | solution.py:263
  122.6 2.5 %projections.1 = bf16[4,272,256]{2,1,0:T(8,128)(2,1)} custom-call(s32[1]{0:T(128)} %bitcast.line_ref, bf16[2560,128]{1,0:T(8,128)(2,1)S(1)} %get-tuple-element.20.refs_0_, bf16[2560,128]{1,0:T(8,128)(2,1)S(1)} %collective-permute-done.refs_1_, bf16[2560,128]{1,0:T(8,128)(2,1)S(1)} %collective-permute-done.1.refs_2_, ...), custom_call_target="tpu_custom_call" | custom-call | tf_op jit(solution)/shard_map/projections/pallas_call | solution.py:43
  125.2 4.8 %all-to-all-start.1 = ((bf16[4,272,256]{2,1,0:T(8,128)(2,1)}), bf16[4,272,256]{2,1,0:T(8,128)(2,1)S(1)}, u32[]{:S(2)}, u32[]{:S(2)}) async-start(bf16[4,272,256]{2,1,0:T(8,128)(2,1)} %projections.1), calls=%async_computation.1 | async-start | bytes 1114112 | tf_op jit(solution)/shard_map/all_to_all | solution.py:24
  130.3 7.9 %all-to-all-done.1.got_ref = bf16[4,272,256]{2,1,0:T(8,128)(2,1)S(1)} async-done(((bf16[4,272,256]{2,1,0:T(8,128)(2,1)}), bf16[4,272,256]{2,1,0:T(8,128)(2,1)S(1)}, u32[]{:S(2)}, u32[]{:S(2)}) %all-to-all-start.1) | async-done | bytes 557088 | tf_op jit(solution)/shard_map/all_to_all | solution.py:24
  138.4 16.9 %all_to_all.15.pairs_ref = bf16[8,32,256]{2,1,0:T(8,128)(2,1)S(1)} all-to-all(bf16[8,32,256]{2,1,0:T(8,128)(2,1)S(1)} %get-tuple-element.16), channel_id=1, replica_groups=mesh['section'=16,'b'=4,'z'=2,'y'=4] {'b','z'}, dimensions={0} | all-to-all | bytes 262144 | tf_op jit(solution)/shard_map/all_to_all | solution.py:24
  155.3 1.2 attention.1
  (23 shorter events, 2.0 us)
Async XLA Ops:
  0.0 1.6 %copy-start.1 = (bf16[1,128,8192]{2,1,0:T(8,128)(2,1)S(1)}, bf16[1,128,8192]{2,1,0:T(8,128)(2,1)}, u32[]{:S(2)}) copy-start(bf16[1,128,8192]{2,1,0:T(8,128)(2,1)} %weight.1) | copy-start | bytes 6291460
  1.6 0.8 copy-start.3
  3.3 1.5 copy-start
  4.8 37.5 %all-to-all-start = ((bf16[8,128,1280]{2,1,0:T(8,128)(2,1)}), bf16[8,128,1280]{2,1,0:T(8,128)(2,1)S(1)}, u32[]{:S(2)}, u32[]{:S(2)}) async-start(bf16[8,128,1280]{2,1,0:T(8,128)(2,1)} %copy-done), calls=%async_computation | async-start | bytes 5242880 | tf_op jit(solution)/shard_map/all_to_all | solution.py:24
  11.2 31.1 %copy-start.2 = (bf16[1,256,256]{2,1,0:T(8,128)(2,1)S(1)}, bf16[1,256,256]{2,1,0:T(8,128)(2,1)}, u32[]{:S(2)}) copy-start(bf16[1,256,256]{2,1,0:T(8,128)(2,1)} %residual_ref.1) | copy-start | bytes 393220
  42.3 23.4 %copy-start.4 = (bf16[4,2560,128]{2,1,0:T(8,128)(2,1)S(1)}, bf16[4,2560,128]{2,1,0:T(8,128)(2,1)}, u32[]{:S(2)}) copy-start(bf16[4,2560,128]{2,1,0:T(8,128)(2,1)} %in_pieces.1) | copy-start | bytes 7864324
  43.1 26.1 %collective-permute-start.3 = (bf16[256,256]{1,0:T(8,128)(2,1)S(1)}, bf16[256,256]{1,0:T(8,128)(2,1)S(1)}, u32[]{:S(2)}, u32[]{:S(2)}) collective-permute-start(bf16[256,256]{1,0:T(8,128)(2,1)S(1)} %get-tuple-element.11), channel_id=1, source_target_pairs={{0,48},{8,56},{16,32},{24,40},{32,80},{40,88},{48,64},{56,72},{64,... | collective-permute-start | bytes 393224 | tf_op jit(solution)/shard_map/ppermute | solution.py:246
  51.6 21.9 %collective-permute-start.4 = (bf16[256,256]{1,0:T(8,128)(2,1)S(1)}, bf16[256,256]{1,0:T(8,128)(2,1)S(1)}, u32[]{:S(2)}, u32[]{:S(2)}) collective-permute-start(bf16[256,256]{1,0:T(8,128)(2,1)S(1)} %get-tuple-element.12), channel_id=1, source_target_pairs={{0,56},{8,48},{16,40},{24,32},{32,88},{40,80},{48,72},{56,64},{64,... | collective-permute-start | bytes 393224 | tf_op jit(solution)/shard_map/ppermute | solution.py:246
  61.1 16.4 %collective-permute-start.5 = (bf16[256,256]{1,0:T(8,128)(2,1)S(1)}, bf16[256,256]{1,0:T(8,128)(2,1)S(1)}, u32[]{:S(2)}, u32[]{:S(2)}) collective-permute-start(bf16[256,256]{1,0:T(8,128)(2,1)S(1)} %get-tuple-element.13), channel_id=1, source_target_pairs={{0,40},{8,32},{16,56},{24,48},{32,72},{40,64},{48,88},{56,80},{64,... | collective-permute-start | bytes 393224 | tf_op jit(solution)/shard_map/ppermute | solution.py:246
  63.8 5.3 %copy-start.5 = (f32[1,256]{1,0:T(1,128)S(1)}, f32[1,256]{1,0:T(1,128)}, u32[]{:S(2)}) copy-start(f32[1,256]{1,0:T(1,128)} %param.9) | copy-start | bytes 3076
  63.8 22.3 %collective-permute-start.6 = (bf16[256,256]{1,0:T(8,128)(2,1)S(1)}, bf16[256,256]{1,0:T(8,128)(2,1)S(1)}, u32[]{:S(2)}, u32[]{:S(2)}) collective-permute-start(bf16[256,256]{1,0:T(8,128)(2,1)S(1)} %get-tuple-element.14), channel_id=1, source_target_pairs={{0,32},{8,40},{16,48},{24,56},{32,64},{40,72},{48,80},{56,88},{64,... | collective-permute-start | bytes 393224 | tf_op jit(solution)/shard_map/ppermute | solution.py:246
  67.0 46.2 %collective-permute-start = (bf16[2560,128]{1,0:T(8,128)(2,1)}, bf16[2560,128]{1,0:T(8,128)(2,1)S(1)}, u32[]{:S(2)}, u32[]{:S(2)}) collective-permute-start(bf16[2560,128]{1,0:T(8,128)(2,1)} %get-tuple-element.19), channel_id=1, source_target_pairs={{0,1},{1,0},{2,3},{3,2},{4,5},{5,4},{6,7},{7,6},{8,9},{9,8},{10,11... | collective-permute-start | bytes 1966088 | tf_op jit(solution)/shard_map/ppermute | solution.py:254
  69.2 44.0 %collective-permute-start.1 = (bf16[2560,128]{1,0:T(8,128)(2,1)}, bf16[2560,128]{1,0:T(8,128)(2,1)S(1)}, u32[]{:S(2)}, u32[]{:S(2)}) collective-permute-start(bf16[2560,128]{1,0:T(8,128)(2,1)} %get-tuple-element.18), channel_id=1, source_target_pairs={{0,2},{1,3},{2,0},{3,1},{4,6},{5,7},{6,4},{7,5},{8,10},{9,11},{10,... | collective-permute-start | bytes 1966088 | tf_op jit(solution)/shard_map/ppermute | solution.py:254
  73.5 39.7 %collective-permute-start.2 = (bf16[2560,128]{1,0:T(8,128)(2,1)S(1)}, bf16[2560,128]{1,0:T(8,128)(2,1)S(1)}, u32[]{:S(2)}, u32[]{:S(2)}) collective-permute-start(bf16[2560,128]{1,0:T(8,128)(2,1)S(1)} %get-tuple-element.17), channel_id=1, source_target_pairs={{0,3},{1,2},{2,1},{3,0},{4,7},{5,6},{6,5},{7,4},{8,11},{9,10},{10,... | collective-permute-start | bytes 1966088 | tf_op jit(solution)/shard_map/ppermute | solution.py:254
  111.2 11.4 %collective-permute-start.7 = (bf16[4,272,256]{2,1,0:T(8,128)(2,1)S(1)}, bf16[4,272,256]{2,1,0:T(8,128)(2,1)S(1)}, u32[]{:S(2)}, u32[]{:S(2)}) collective-permute-start(bf16[4,272,256]{2,1,0:T(8,128)(2,1)S(1)} %bitcast.16), channel_id=1, source_target_pairs={{0,4},{4,0},{1,5},{5,1},{2,6},{6,2},{3,7},{7,3},{8,12},{12,8},{9,1... | collective-permute-start | bytes 1671176 | tf_op jit(solution)/shard_map/ppermute | solution.py:263
  125.2 13.1 %all-to-all-start.1 = ((bf16[4,272,256]{2,1,0:T(8,128)(2,1)}), bf16[4,272,256]{2,1,0:T(8,128)(2,1)S(1)}, u32[]{:S(2)}, u32[]{:S(2)}) async-start(bf16[4,272,256]{2,1,0:T(8,128)(2,1)} %projections.1), calls=%async_computation.1 | async-start | bytes 1114112 | tf_op jit(solution)/shard_map/all_to_all | solution.py:24

commit v6 on v5

--- a/solution.py
+++ b/solution.py
@@ -258,7 +258,7 @@
     angles = frequency[:, None] * positions[None, :]
     cosine, sine = jnp.cos(angles), jnp.sin(angles)
 
-    received = [to_row(terms[k], k, 1) for k in (2, 3, 1, 0)]
+    received = [to_row(terms[k], k, 1) for k in (2, 3, 0, 1)]
     gathered = lax.all_gather(scaled_sum(received, gain.T), "b", axis=0)
     other = lax.ppermute(gathered, "z", [(0, 1), (1, 0)])
     summed = exchange(projections(weights, gathered, other, line), "y")

time: 160 us -> 159 us (level); the launches traced: 157 us -> 158 us
  waiting for transfers between devices: 52 us -> 43 us
  starting transfers between devices: 45.6 us -> 51.5 us
  blocking collectives: 42 us -> 46.3 us
    ppermute x4, waiting for transfers between devices: 8.51 us -> 1.47 us  [to_row(): return lax.ppermute(piece, ('section', 'b'), route)]
    ppermute x1, starting transfers between devices: 1.91 us -> 6.57 us  [on_device(): other = lax.ppermute(gathered, 'z', [(0, 1), (1, 0)])]
    all_gather x1, blocking collectives: 25 us -> 27.2 us  [on_device(): gathered = lax.all_gather(scaled_sum(received, gain.T), 'b', axis=0)]
    all_to_all x1, blocking collectives: 16.9 us -> 19.1 us  [exchange(): return lax.all_to_all(pieces, axis, 0, 0, tiled=True)]
    ppermute x1, waiting for transfers between devices: 9.47 us -> 7.46 us  [on_device(): other = lax.ppermute(gathered, 'z', [(0, 1), (1, 0)])]
where the time goes in v6:
time: 159 us; the launch traced here: 158 us
  starting transfers between devices  51.5 us (32%)
  blocking collectives  46.3 us (29%)
  waiting for transfers between devices  43 us (27%)
  Pallas kernels  10.5 us (7%)
  local copies, waits for them, and re-layouts  5.32 us (3%)
    all_to_all x2, waiting for transfers between devices, exchange(): return lax.all_to_all(pieces, axis, 0, 0, tiled=True)  34 us
    all_gather x1, blocking collectives, on_device(): gathered = lax.all_gather(scaled_sum(received, gain.T), 'b', axis=0)  27.2 us
    ppermute x4, starting transfers between devices, to_row(): return lax.ppermute(piece, ('section', 'b'), route)  23.5 us
    all_to_all x1, blocking collectives, exchange(): return lax.all_to_all(pieces, axis, 0, 0, tiled=True)  19.1 us
    all_to_all x2, starting transfers between devices, exchange(): return lax.all_to_all(pieces, axis, 0, 0, tiled=True)  11 us
    ppermute x3, starting transfers between devices, on_device(): lax.ppermute(pieces[k], 'y', [(y, y ^ k) for y in range(LINE)])  10.4 us
    ppermute x1, waiting for transfers between devices, on_device(): other = lax.ppermute(gathered, 'z', [(0, 1), (1, 0)])  7.46 us
    ppermute x1, starting transfers between devices, on_device(): other = lax.ppermute(gathered, 'z', [(0, 1), (1, 0)])  6.57 us
  transfers between devices with their start and end apart: 10, of which 4 were waited for; matrix products, arithmetic and copies ran while one was open for 1% of the time, Pallas kernels for 3%

profile of v6, /device:TPU:6, one launch (start us, length us, event | category | flops | bytes accessed | tf_op | source)
XLA Modules:
  0.0 157.7 jit_solution(13574028412416843779)
XLA Ops:
  0.0 1.6 %copy-done.1 = bf16[1,128,8192]{2,1,0:T(8,128)(2,1)S(1)} copy-done((bf16[1,128,8192]{2,1,0:T(8,128)(2,1)S(1)}, bf16[1,128,8192]{2,1,0:T(8,128)(2,1)}, u32[]{:S(2)}) %copy-start.1) | copy-done | bytes 2097176
  1.6 0.8 copy-done.3
  2.4 0.9 out_pieces.1
  3.3 1.5 copy-done
  4.8 5.8 %all-to-all-start = ((bf16[8,128,1280]{2,1,0:T(8,128)(2,1)}), bf16[8,128,1280]{2,1,0:T(8,128)(2,1)S(1)}, u32[]{:S(2)}, u32[]{:S(2)}) async-start(bf16[8,128,1280]{2,1,0:T(8,128)(2,1)} %copy-done), calls=%async_computation | async-start | bytes 5242880 | tf_op jit(solution)/shard_map/all_to_all | solution.py:24
  11.2 5.0 %in_pieces.1 = bf16[4,2560,128]{2,1,0:T(8,128)(2,1)} custom-call(s32[2]{0:T(128)} %pad_add_fusion.side_ref, bf16[1,8192,128]{2,1,0:T(8,128)(2,1)} %refs_7_.1, bf16[1,8192,128]{2,1,0:T(8,128)(2,1)} %refs_7_.1, bf16[1,8192,128]{2,1,0:T(8,128)(2,1)} %refs_7_.1, bf16[1,8192,128]{2,1,0:T(8,128)(2,1)} %refs_7_.1, bf16[1,8192,128]{2,1,0:T(8,128)(2,1)} %refs_7_.1, ...), custom_call_target="tpu_custom_call" | custom-call | tf_op jit(solution)/shard_map/in_pieces/pallas_call | solution.py:101
  16.2 26.1 %all-to-all-done.got_ref = bf16[8,128,1280]{2,1,0:T(8,128)(2,1)S(1)} async-done(((bf16[8,128,1280]{2,1,0:T(8,128)(2,1)}), bf16[8,128,1280]{2,1,0:T(8,128)(2,1)S(1)}, u32[]{:S(2)}, u32[]{:S(2)}) %all-to-all-start) | async-done | bytes 2621472 | tf_op jit(solution)/shard_map/all_to_all | solution.py:24
  43.1 8.5 %collective-permute-start.3 = (bf16[256,256]{1,0:T(8,128)(2,1)S(1)}, bf16[256,256]{1,0:T(8,128)(2,1)S(1)}, u32[]{:S(2)}, u32[]{:S(2)}) collective-permute-start(bf16[256,256]{1,0:T(8,128)(2,1)S(1)} %get-tuple-element.11), channel_id=1, source_target_pairs={{0,48},{8,56},{16,32},{24,40},{32,80},{40,88},{48,64},{56,72},{64,... | collective-permute-start | bytes 393224 | tf_op jit(solution)/shard_map/ppermute | solution.py:246
  51.6 9.6 %collective-permute-start.4 = (bf16[256,256]{1,0:T(8,128)(2,1)S(1)}, bf16[256,256]{1,0:T(8,128)(2,1)S(1)}, u32[]{:S(2)}, u32[]{:S(2)}) collective-permute-start(bf16[256,256]{1,0:T(8,128)(2,1)S(1)} %get-tuple-element.12), channel_id=1, source_target_pairs={{0,56},{8,48},{16,40},{24,32},{32,88},{40,80},{48,72},{56,64},{64,... | collective-permute-start | bytes 393224 | tf_op jit(solution)/shard_map/ppermute | solution.py:246
  61.1 1.9 %collective-permute-start.5 = (bf16[256,256]{1,0:T(8,128)(2,1)S(1)}, bf16[256,256]{1,0:T(8,128)(2,1)S(1)}, u32[]{:S(2)}, u32[]{:S(2)}) collective-permute-start(bf16[256,256]{1,0:T(8,128)(2,1)S(1)} %get-tuple-element.13), channel_id=1, source_target_pairs={{0,32},{8,40},{16,48},{24,56},{32,64},{40,72},{48,80},{56,88},{64,... | collective-permute-start | bytes 393224 | tf_op jit(solution)/shard_map/ppermute | solution.py:246
  63.1 3.6 %collective-permute-start.6 = (bf16[256,256]{1,0:T(8,128)(2,1)S(1)}, bf16[256,256]{1,0:T(8,128)(2,1)S(1)}, u32[]{:S(2)}, u32[]{:S(2)}) collective-permute-start(bf16[256,256]{1,0:T(8,128)(2,1)S(1)} %get-tuple-element.14), channel_id=1, source_target_pairs={{0,40},{8,32},{16,56},{24,48},{32,72},{40,64},{48,88},{56,80},{64,... | collective-permute-start | bytes 393224 | tf_op jit(solution)/shard_map/ppermute | solution.py:246
  66.6 1.2 slice_bitcast_fusion
  67.9 2.1 %collective-permute-start = (bf16[2560,128]{1,0:T(8,128)(2,1)}, bf16[2560,128]{1,0:T(8,128)(2,1)S(1)}, u32[]{:S(2)}, u32[]{:S(2)}) collective-permute-start(bf16[2560,128]{1,0:T(8,128)(2,1)} %get-tuple-element.19), channel_id=1, source_target_pairs={{0,1},{1,0},{2,3},{3,2},{4,5},{5,4},{6,7},{7,6},{8,9},{9,8},{10,11... | collective-permute-start | bytes 1966088 | tf_op jit(solution)/shard_map/ppermute | solution.py:254
  70.2 4.0 %collective-permute-start.1 = (bf16[2560,128]{1,0:T(8,128)(2,1)}, bf16[2560,128]{1,0:T(8,128)(2,1)S(1)}, u32[]{:S(2)}, u32[]{:S(2)}) collective-permute-start(bf16[2560,128]{1,0:T(8,128)(2,1)} %get-tuple-element.18), channel_id=1, source_target_pairs={{0,2},{1,3},{2,0},{3,1},{4,6},{5,7},{6,4},{7,5},{8,10},{9,11},{10,... | collective-permute-start | bytes 1966088 | tf_op jit(solution)/shard_map/ppermute | solution.py:254
  74.3 4.2 %collective-permute-start.2 = (bf16[2560,128]{1,0:T(8,128)(2,1)S(1)}, bf16[2560,128]{1,0:T(8,128)(2,1)S(1)}, u32[]{:S(2)}, u32[]{:S(2)}) collective-permute-start(bf16[2560,128]{1,0:T(8,128)(2,1)S(1)} %get-tuple-element.17), channel_id=1, source_target_pairs={{0,3},{1,2},{2,1},{3,0},{4,7},{5,6},{6,5},{7,4},{8,11},{9,10},{10,... | collective-permute-start | bytes 1966088 | tf_op jit(solution)/shard_map/ppermute | solution.py:254
  78.5 1.4 collective-permute-done.5.refs_2_
  80.1 27.2 %all-gather = bf16[1088,256]{1,0:T(8,128)(2,1)S(1)} all-gather(bf16[272,256]{1,0:T(8,128)(2,1)S(1)} %scaled_sum.1), channel_id=2, replica_groups=mesh['section'=16,'b'=4,'z'=2,'y'=4] {'b'}, dimensions={0}, use_global_device_ids=true | all-gather | bytes 696320 | tf_op jit(solution)/shard_map/all_gather | solution.py:262
  107.3 6.6 %collective-permute-start.7 = (bf16[4,272,256]{2,1,0:T(8,128)(2,1)S(1)}, bf16[4,272,256]{2,1,0:T(8,128)(2,1)S(1)}, u32[]{:S(2)}, u32[]{:S(2)}) collective-permute-start(bf16[4,272,256]{2,1,0:T(8,128)(2,1)S(1)} %bitcast.16), channel_id=1, source_target_pairs={{0,4},{4,0},{1,5},{5,1},{2,6},{6,2},{3,7},{7,3},{8,12},{12,8},{9,1... | collective-permute-start | bytes 1671176 | tf_op jit(solution)/shard_map/ppermute | solution.py:263
  113.9 7.5 %collective-permute-done.7.refs_5_ = bf16[4,272,256]{2,1,0:T(8,128)(2,1)S(1)} collective-permute-done((bf16[4,272,256]{2,1,0:T(8,128)(2,1)S(1)}, bf16[4,272,256]{2,1,0:T(8,128)(2,1)S(1)}, u32[]{:S(2)}, u32[]{:S(2)}) %collective-permute-start.7) | collective-permute-done | bytes 557088 | tf_op jit(solution)/shard_map/ppermute | solution.py:263
  121.4 2.5 %projections.1 = bf16[4,272,256]{2,1,0:T(8,128)(2,1)} custom-call(s32[1]{0:T(128)} %bitcast.line_ref, bf16[2560,128]{1,0:T(8,128)(2,1)S(1)} %get-tuple-element.20.refs_0_, bf16[2560,128]{1,0:T(8,128)(2,1)S(1)} %collective-permute-done.refs_1_, bf16[2560,128]{1,0:T(8,128)(2,1)S(1)} %collective-permute-done.1.refs_2_, ...), custom_call_target="tpu_custom_call" | custom-call | tf_op jit(solution)/shard_map/projections/pallas_call | solution.py:43
  123.9 5.2 %all-to-all-start.1 = ((bf16[4,272,256]{2,1,0:T(8,128)(2,1)}), bf16[4,272,256]{2,1,0:T(8,128)(2,1)S(1)}, u32[]{:S(2)}, u32[]{:S(2)}) async-start(bf16[4,272,256]{2,1,0:T(8,128)(2,1)} %projections.1), calls=%async_computation.1 | async-start | bytes 1114112 | tf_op jit(solution)/shard_map/all_to_all | solution.py:24
  129.4 7.9 %all-to-all-done.1.got_ref = bf16[4,272,256]{2,1,0:T(8,128)(2,1)S(1)} async-done(((bf16[4,272,256]{2,1,0:T(8,128)(2,1)}), bf16[4,272,256]{2,1,0:T(8,128)(2,1)S(1)}, u32[]{:S(2)}, u32[]{:S(2)}) %all-to-all-start.1) | async-done | bytes 557088 | tf_op jit(solution)/shard_map/all_to_all | solution.py:24
  137.4 19.1 %all_to_all.15.pairs_ref = bf16[8,32,256]{2,1,0:T(8,128)(2,1)S(1)} all-to-all(bf16[8,32,256]{2,1,0:T(8,128)(2,1)S(1)} %get-tuple-element.16), channel_id=1, replica_groups=mesh['section'=16,'b'=4,'z'=2,'y'=4] {'b','z'}, dimensions={0} | all-to-all | bytes 262144 | tf_op jit(solution)/shard_map/all_to_all | solution.py:24
  156.5 1.2 attention.1
  (23 shorter events, 2.1 us)
Async XLA Ops:
  0.0 1.6 %copy-start.1 = (bf16[1,128,8192]{2,1,0:T(8,128)(2,1)S(1)}, bf16[1,128,8192]{2,1,0:T(8,128)(2,1)}, u32[]{:S(2)}) copy-start(bf16[1,128,8192]{2,1,0:T(8,128)(2,1)} %weight.1) | copy-start | bytes 6291460
  1.6 0.8 copy-start.3
  3.3 1.5 copy-start
  4.8 37.5 %all-to-all-start = ((bf16[8,128,1280]{2,1,0:T(8,128)(2,1)}), bf16[8,128,1280]{2,1,0:T(8,128)(2,1)S(1)}, u32[]{:S(2)}, u32[]{:S(2)}) async-start(bf16[8,128,1280]{2,1,0:T(8,128)(2,1)} %copy-done), calls=%async_computation | async-start | bytes 5242880 | tf_op jit(solution)/shard_map/all_to_all | solution.py:24
  11.2 31.1 %copy-start.2 = (bf16[1,256,256]{2,1,0:T(8,128)(2,1)S(1)}, bf16[1,256,256]{2,1,0:T(8,128)(2,1)}, u32[]{:S(2)}) copy-start(bf16[1,256,256]{2,1,0:T(8,128)(2,1)} %residual_ref.1) | copy-start | bytes 393220
  42.3 24.4 %copy-start.4 = (bf16[4,2560,128]{2,1,0:T(8,128)(2,1)S(1)}, bf16[4,2560,128]{2,1,0:T(8,128)(2,1)}, u32[]{:S(2)}) copy-start(bf16[4,2560,128]{2,1,0:T(8,128)(2,1)} %in_pieces.1) | copy-start | bytes 7864324
  43.1 27.1 %collective-permute-start.3 = (bf16[256,256]{1,0:T(8,128)(2,1)S(1)}, bf16[256,256]{1,0:T(8,128)(2,1)S(1)}, u32[]{:S(2)}, u32[]{:S(2)}) collective-permute-start(bf16[256,256]{1,0:T(8,128)(2,1)S(1)} %get-tuple-element.11), channel_id=1, source_target_pairs={{0,48},{8,56},{16,32},{24,40},{32,80},{40,88},{48,64},{56,72},{64,... | collective-permute-start | bytes 393224 | tf_op jit(solution)/shard_map/ppermute | solution.py:246
  51.6 22.7 %collective-permute-start.4 = (bf16[256,256]{1,0:T(8,128)(2,1)S(1)}, bf16[256,256]{1,0:T(8,128)(2,1)S(1)}, u32[]{:S(2)}, u32[]{:S(2)}) collective-permute-start(bf16[256,256]{1,0:T(8,128)(2,1)S(1)} %get-tuple-element.12), channel_id=1, source_target_pairs={{0,56},{8,48},{16,40},{24,32},{32,88},{40,80},{48,72},{56,64},{64,... | collective-permute-start | bytes 393224 | tf_op jit(solution)/shard_map/ppermute | solution.py:246
  61.1 18.8 %collective-permute-start.5 = (bf16[256,256]{1,0:T(8,128)(2,1)S(1)}, bf16[256,256]{1,0:T(8,128)(2,1)S(1)}, u32[]{:S(2)}, u32[]{:S(2)}) collective-permute-start(bf16[256,256]{1,0:T(8,128)(2,1)S(1)} %get-tuple-element.13), channel_id=1, source_target_pairs={{0,32},{8,40},{16,48},{24,56},{32,64},{40,72},{48,80},{56,88},{64,... | collective-permute-start | bytes 393224 | tf_op jit(solution)/shard_map/ppermute | solution.py:246
  63.1 7.0 %copy-start.5 = (f32[1,256]{1,0:T(1,128)S(1)}, f32[1,256]{1,0:T(1,128)}, u32[]{:S(2)}) copy-start(f32[1,256]{1,0:T(1,128)} %param.9) | copy-start | bytes 3076
  63.1 16.9 %collective-permute-start.6 = (bf16[256,256]{1,0:T(8,128)(2,1)S(1)}, bf16[256,256]{1,0:T(8,128)(2,1)S(1)}, u32[]{:S(2)}, u32[]{:S(2)}) collective-permute-start(bf16[256,256]{1,0:T(8,128)(2,1)S(1)} %get-tuple-element.14), channel_id=1, source_target_pairs={{0,40},{8,32},{16,56},{24,48},{32,72},{40,64},{48,88},{56,80},{64,... | collective-permute-start | bytes 393224 | tf_op jit(solution)/shard_map/ppermute | solution.py:246
  67.9 46.0 %collective-permute-start = (bf16[2560,128]{1,0:T(8,128)(2,1)}, bf16[2560,128]{1,0:T(8,128)(2,1)S(1)}, u32[]{:S(2)}, u32[]{:S(2)}) collective-permute-start(bf16[2560,128]{1,0:T(8,128)(2,1)} %get-tuple-element.19), channel_id=1, source_target_pairs={{0,1},{1,0},{2,3},{3,2},{4,5},{5,4},{6,7},{7,6},{8,9},{9,8},{10,11... | collective-permute-start | bytes 1966088 | tf_op jit(solution)/shard_map/ppermute | solution.py:254
  70.2 43.7 %collective-permute-start.1 = (bf16[2560,128]{1,0:T(8,128)(2,1)}, bf16[2560,128]{1,0:T(8,128)(2,1)S(1)}, u32[]{:S(2)}, u32[]{:S(2)}) collective-permute-start(bf16[2560,128]{1,0:T(8,128)(2,1)} %get-tuple-element.18), channel_id=1, source_target_pairs={{0,2},{1,3},{2,0},{3,1},{4,6},{5,7},{6,4},{7,5},{8,10},{9,11},{10,... | collective-permute-start | bytes 1966088 | tf_op jit(solution)/shard_map/ppermute | solution.py:254
  74.3 39.6 %collective-permute-start.2 = (bf16[2560,128]{1,0:T(8,128)(2,1)S(1)}, bf16[2560,128]{1,0:T(8,128)(2,1)S(1)}, u32[]{:S(2)}, u32[]{:S(2)}) collective-permute-start(bf16[2560,128]{1,0:T(8,128)(2,1)S(1)} %get-tuple-element.17), channel_id=1, source_target_pairs={{0,3},{1,2},{2,1},{3,0},{4,7},{5,6},{6,5},{7,4},{8,11},{9,10},{10,... | collective-permute-start | bytes 1966088 | tf_op jit(solution)/shard_map/ppermute | solution.py:254
  107.3 14.1 %collective-permute-start.7 = (bf16[4,272,256]{2,1,0:T(8,128)(2,1)S(1)}, bf16[4,272,256]{2,1,0:T(8,128)(2,1)S(1)}, u32[]{:S(2)}, u32[]{:S(2)}) collective-permute-start(bf16[4,272,256]{2,1,0:T(8,128)(2,1)S(1)} %bitcast.16), channel_id=1, source_target_pairs={{0,4},{4,0},{1,5},{5,1},{2,6},{6,2},{3,7},{7,3},{8,12},{12,8},{9,1... | collective-permute-start | bytes 1671176 | tf_op jit(solution)/shard_map/ppermute | solution.py:263
  123.9 13.4 %all-to-all-start.1 = ((bf16[4,272,256]{2,1,0:T(8,128)(2,1)}), bf16[4,272,256]{2,1,0:T(8,128)(2,1)S(1)}, u32[]{:S(2)}, u32[]{:S(2)}) async-start(bf16[4,272,256]{2,1,0:T(8,128)(2,1)} %projections.1), calls=%async_computation.1 | async-start | bytes 1114112 | tf_op jit(solution)/shard_map/all_to_all | solution.py:24
